TPU v7x, 32 devices: a whole 2x2x4 slice. The times are simulated.
32 devices in a mesh: dp: 16 (over z, x, core), mp: 2 (over y).
Axes of the slice: x: 2, y: 2, z: 4, core: 2. Of those that a mesh axis runs over, the one named last changes fastest.
Arguments:
- tokens: bfloat16 [16384, 1024], P(('dp', 'mp')), may hold values from -6 to 6
- lengths: int32 [16], P('dp'), may hold values from 512 to 1024, as said below
- first_gain: float32 [1024], replicated, may hold values from 0.5 to 1.5
- first_shift: float32 [1024], replicated, may hold values from -1 to 1
- heads_weight: bfloat16 [3, 1024, 1024], P(None, None, 'mp'), may hold values from -0.1875 to 0.1875
- relative_bias: float32 [16, 32], P('mp'), may hold values from -4 to 4
- mixer_weight: bfloat16 [1024, 1024], P('mp'), may hold values from -0.5 to 0.5
- second_gain: float32 [1024], replicated, may hold values from 0.5 to 1.5
- second_shift: float32 [1024], replicated, may hold values from -1 to 1
- expand_weight: bfloat16 [1024, 4096], P(None, 'mp'), may hold values from -0.1875 to 0.1875
- expand_bias: bfloat16 [4096], P('mp'), may hold values from -3 to 3
- reduce_weight: bfloat16 [4096, 1024], P('mp'), may hold values from -0.09375 to 0.09375
- reduce_bias: float32 [1024], replicated, may hold values from -1.5 to 1.5
- cotangent: bfloat16 [16384, 1024], P(('dp', 'mp')), may hold values from -6 to 6
Outputs:
- block_out: bfloat16 [16384, 1024], P(('dp', 'mp'))
- tokens_grad: bfloat16 [16384, 1024], P(('dp', 'mp'))
- first_gain_grad: float32 [1024], replicated
- first_shift_grad: float32 [1024], replicated
- heads_weight_grad: float32 [3, 1024, 1024], P(None, None, 'mp')
- relative_bias_grad: float32 [16, 32], P('mp')
- mixer_weight_grad: float32 [1024, 1024], P('mp')
- second_gain_grad: float32 [1024], replicated
- second_shift_grad: float32 [1024], replicated
- expand_weight_grad: float32 [1024, 4096], P(None, 'mp')
- expand_bias_grad: float32 [4096], P('mp')
- reduce_weight_grad: float32 [4096, 1024], P('mp')
- reduce_bias_grad: float32 [1024], replicated
Inputs may be any that keep to these rules, and one draw needn't show every extreme that they name: Each sequence holds lengths valid tokens followed by padding slots; some sequence fills all 1024 slots.
All inputs are finite; a program needn't handle non-finite values.
Results may differ from a plain program's by a relative error of at most 0.025.
Values may be sent and summed in bfloat16 or wider, within the bound.
No kernel may reach another device: no remote copies, remote signals or barrier semaphores. Data moves between devices by JAX's collectives and lax.ppermute only.
A program may use at most 320 MiB of HBM per device.

v0:
```python
import functools
import math

import jax
import jax.numpy as jnp
import numpy as np
from jax import lax
from jax.experimental import pallas as pl
from jax.experimental.pallas import tpu as pltpu
from jax.sharding import PartitionSpec as P

EPS = 1e-05
DH=64; MAXDIST=128; NEG=-1e30; BLK=256
F32=jnp.float32; BF16=jnp.bfloat16
HIGHEST=lax.Precision.HIGHEST

def bucket_table(count, buckets, reach):
    exact = buckets // 2
    entries = []
    for position in range(count):
        if position < exact:
            entries.append(position)
        else:
            level = exact + int(math.log(position / exact) / math.log(reach / exact) * (buckets - exact))
            entries.append(min(buckets - 1, level))
    return np.array(entries, dtype=np.int32)

def bias_tables(buckets):
    W=2*BLK
    tab=bucket_table(W,buckets,MAXDIST)
    oh=np.zeros((buckets,4,W),np.float32); neg=np.zeros((1,4,W),np.float32)
    for y in range(W):
        x = y if y < BLK else y-W
        if x<=0 and -x<BLK: oh[tab[-x],0,y]=1
        else: neg[0,0,y]=NEG
        d=BLK-x
        if 0<=d<W: oh[tab[d],1,y]=1
        if 0<=x: oh[tab[x],2,y]=1
        else: neg[0,2,y]=NEG
        d=BLK+x
        if 0<=d<W: oh[tab[d],3,y]=1
    return oh.reshape(buckets,4*W), neg.reshape(1,4*W)

def bias_rows(relative_bias):
    heads,buckets=relative_bias.shape
    oh,neg=bias_tables(buckets)
    rel=relative_bias-relative_bias[:,buckets-1:]
    rows=jnp.dot(rel,jnp.asarray(oh),precision=HIGHEST)+jnp.asarray(neg)
    return rows.reshape(heads//2,2,4*2*BLK)

def split3(x):
    hi=x.astype(BF16); rest=x-hi.astype(F32); mid=rest.astype(BF16)
    lo=(rest-mid.astype(F32)).astype(BF16)
    return hi.astype(F32),mid.astype(F32),lo.astype(F32)

def toeplitz(row):
    wide=jnp.broadcast_to(row,(BLK,2*BLK))
    return pltpu.roll(wide,0,1,stride=1,stride_axis=0)[:,:BLK]

def halves(ref, off, half, lead=()):
    lo=ref[(*lead, pl.ds(pl.multiple_of(off,half),half), slice(None))]
    hi=ref[(*lead, pl.ds(pl.multiple_of(half-off,half),half), slice(None))]
    return lo,hi

def fwd_kernel(sp, q_ref,k_ref,v_ref,b_ref,o_ref,lse_ref,qs,ks,vs):
    T=q_ref.shape[1]; half=T//2; off=pl.multiple_of(sp[0],half); length=sp[1]
    lane=lax.broadcasted_iota(jnp.int32,(1,128),1)
    W=2*BLK
    for part in range(2):
        start=pl.multiple_of(off if part==0 else half-off, half)
        rows=pl.ds(start,half)
        q=q_ref[0,rows,:].astype(F32); k=k_ref[0,rows,:].astype(F32); v=v_ref[0,rows,:].astype(F32)
        pos=lax.broadcasted_iota(jnp.int32,(half,1),0)+part*half
        gone=jnp.where(pos<length,0.0,NEG).astype(F32)
        for h in range(2):
            mine=(lane//DH)==h
            spare=lane==(DH*(1-h))
            dst=slice(part*half,(part+1)*half)
            qs[h,dst,:]=jnp.where(mine,q*DH**-0.5,jnp.where(spare,1.0,0.0)).astype(BF16)
            ks[h,dst,:]=jnp.where(mine,k,jnp.where(spare,gone,0.0)).astype(BF16)
            vs[h,dst,:]=jnp.where(mine,v,1.0).astype(BF16)
    for h in range(2):
        mine=(lane//DH)==h
        t0=toeplitz(b_ref[0,h:h+1,0:W]); t1=toeplitz(b_ref[0,h:h+1,W:2*W])
        for i in range(T//BLK):
            kc=(i+1)*BLK
            s=lax.dot_general(qs[h,i*BLK:kc,:],ks[h,:kc,:],(((1,),(1,)),((),())),preferred_element_type=F32)
            parts=[]
            if i>=2: parts.append(s[:,:kc-2*BLK])
            if i>=1: parts.append(s[:,kc-2*BLK:kc-BLK]+t1)
            parts.append(s[:,kc-BLK:]+t0)
            top=functools.reduce(jnp.maximum,[jnp.max(x,axis=1,keepdims=True) for x in parts])
            p=jnp.concatenate([jnp.exp(x-top).astype(BF16) for x in parts],axis=1)
            o=jnp.dot(p,vs[h,:kc,:],preferred_element_type=F32)
            total=o[:,DH*(1-h):DH*(1-h)+1]
            o=o/total
            lse=top+jnp.log(total)
            rows=pl.ds(pl.multiple_of((i*BLK+off)%T,BLK),BLK)
            if h==0:
                o_ref[rows,:]=o.astype(BF16)
                lse_ref[0,rows,:]=jnp.broadcast_to(lse,(BLK,128))
            else:
                o_ref[rows,:]=jnp.where(mine,o,o_ref[rows,:].astype(F32)).astype(BF16)
                lse_ref[0,rows,:]=jnp.where(mine,lse,lse_ref[0,rows,:])

def attend_forward(sp,projected,rows,interpret=False):
    _,T,HD=projected.shape; pairs=HD//128
    return pl.pallas_call(
        fwd_kernel,
        grid_spec=pltpu.PrefetchScalarGridSpec(
            num_scalar_prefetch=1,grid=(pairs,),
            in_specs=[pl.BlockSpec((1,T,128),lambda p,s,c=c:(c,0,p)) for c in range(3)]
              +[pl.BlockSpec((1,2,rows.shape[2]),lambda p,s:(p,0,0))],
            out_specs=[pl.BlockSpec((T,128),lambda p,s:(0,p)),pl.BlockSpec((1,T,128),lambda p,s:(p,0,0))],
            scratch_shapes=[pltpu.VMEM((2,T,128),BF16)]*3),
        out_shape=[jax.ShapeDtypeStruct((T,HD),BF16),jax.ShapeDtypeStruct((pairs,T,128),F32)],
        name="attend_forward",
    )(sp,projected,projected,projected,rows)

def diagonal_sums(acc, offset):
    W=2*BLK
    wide=jnp.concatenate([acc,jnp.zeros_like(acc)],axis=1)
    n=BLK
    while n>1:
        n//=2
        top=wide[:n]; bottom=wide[n:2*n]
        wide=top+pltpu.roll(bottom,W-n,1)
    return pltpu.roll(wide,offset,1) if offset else wide

def bwd_kernel(sp, q_ref,k_ref,v_ref,do_ref,o_ref,lse_ref,b_ref,g_ref,d_ref,qs,ks,vs,dos,dq,acc0,acc1, *, variant):
    T=q_ref.shape[1]; half=T//2; off=pl.multiple_of(sp[0],half); length=sp[1]
    lane=lax.broadcasted_iota(jnp.int32,(1,128),1)
    W=2*BLK
    n=T//BLK
    for part in range(2):
        start=pl.multiple_of(off if part==0 else half-off, half)
        rows=pl.ds(start,half)
        dst=slice(part*half,(part+1)*half)
        q=q_ref[0,rows,:].astype(F32); k=k_ref[0,rows,:].astype(F32); v=v_ref[0,rows,:].astype(F32)
        do=do_ref[rows,:].astype(F32)
        prod=do*o_ref[rows,:].astype(F32)
        lse=lse_ref[0,rows,:]
        pos=lax.broadcasted_iota(jnp.int32,(half,1),0)+part*half
        gone=jnp.where(pos<length,0.0,NEG).astype(F32)
        for h in range(2):
            mine=(lane//DH)==h
            s0=DH*(1-h)
            delta=jnp.sum(jnp.where(mine,prod,0.0),axis=1,keepdims=True)
            dh,dm,dl=split3(delta)
            lh,lm,ll=split3(lse[:,DH*h:DH*h+1])
            def lanes(base,vals):
                out=0.0
                for t,val in enumerate(vals): out=jnp.where(lane==s0+t,val,out)
                return jnp.where(mine,base,out).astype(BF16)
            qs[h,dst,:]=lanes(q*DH**-0.5,(1.0,-lh,-lm,-ll))
            ks[h,dst,:]=lanes(k,(gone,1.0,1.0,1.0))
            vs[h,dst,:]=lanes(v,(1.0,1.0,1.0))
            dos[h,dst,:]=lanes(do,(-dh,-dm,-dl))
    for h in range(2):
        mine=(lane//DH)==h
        t0=toeplitz(b_ref[0,h:h+1,2*W:3*W]); t1=toeplitz(b_ref[0,h:h+1,3*W:])
        for j in range(n):
            cols=slice(j*BLK,T)
            rj=slice(j*BLK,(j+1)*BLK)
            s=lax.dot_general(ks[h,rj,:],qs[h,cols,:],(((1,),(1,)),((),())),preferred_element_type=F32)
            dp=lax.dot_general(vs[h,rj,:],dos[h,cols,:],(((1,),(1,)),((),())),preferred_element_type=F32)
            ps=[];dss=[]
            for b in range(n-j):
                c=slice(b*BLK,(b+1)*BLK)
                x=s[:,c]
                if b==0: x=x+t0
                if b==1: x=x+t1
                p=jnp.exp(x)
                ds=p*dp[:,c]
                if b==0:
                    if j==0: acc0[...]=ds
                    else: acc0[...]+=ds
                if b==1:
                    if j==0: acc1[...]=ds
                    else: acc1[...]+=ds
                ps.append(p.astype(BF16)); dss.append(ds.astype(BF16))
            p=jnp.concatenate(ps,axis=1); ds=jnp.concatenate(dss,axis=1)
            dv=jnp.dot(p,dos[h,cols,:],preferred_element_type=F32)
            dk=jnp.dot(ds,qs[h,cols,:],preferred_element_type=F32)
            kk=jnp.where(mine,ks[h,rj,:].astype(F32),1.0).astype(BF16)
            dqj=lax.dot_general(ds,kk,(((0,),(0,)),((),())),preferred_element_type=F32)
            if j==0: dq[h,:,:]=dqj
            else: dq[h,cols,:]+=dqj
            rows=pl.ds(pl.multiple_of((j*BLK+off)%T,BLK),BLK)
            if h==0:
                g_ref[1,rows,:]=dk.astype(BF16); g_ref[2,rows,:]=dv.astype(BF16)
            else:
                g_ref[1,rows,:]=jnp.where(mine,dk,g_ref[1,rows,:].astype(F32)).astype(BF16)
                g_ref[2,rows,:]=jnp.where(mine,dv,g_ref[2,rows,:].astype(F32)).astype(BF16)
        near=diagonal_sums(acc0[...],0)
        near1=diagonal_sums(acc1[...],BLK)
        d_ref[0,h:h+1,:]=near+near1
        total=jnp.sum(dq[h,:,:],axis=0,keepdims=True)[:,DH*(1-h):DH*(1-h)+1]
        d_ref[0,2+h:3+h,:]=jnp.broadcast_to(total,(1,W))
    first=(lane//DH)==0
    for part in range(2):
        start=pl.multiple_of(off if part==0 else half-off, half)
        dst=slice(part*half,(part+1)*half)
        g_ref[0,pl.ds(start,half),:]=(jnp.where(first,dq[0,dst,:],dq[1,dst,:])*DH**-0.5).astype(BF16)

def attend_backward(sp,projected,grad_mixed,mixed,lse,rows,variant=0):
    _,T,HD=projected.shape; pairs=HD//128
    flat=pl.BlockSpec((T,128),lambda p,s:(0,p))
    return pl.pallas_call(
        functools.partial(bwd_kernel,variant=variant),
        grid_spec=pltpu.PrefetchScalarGridSpec(
            num_scalar_prefetch=1,grid=(pairs,),
            in_specs=[pl.BlockSpec((1,T,128),lambda p,s,c=c:(c,0,p)) for c in range(3)]
              +[flat,flat,pl.BlockSpec((1,T,128),lambda p,s:(p,0,0)),pl.BlockSpec((1,2,rows.shape[2]),lambda p,s:(p,0,0))],
            out_specs=[pl.BlockSpec((3,T,128),lambda p,s:(0,0,p)),pl.BlockSpec((1,4,2*BLK),lambda p,s:(p,0,0))],
            scratch_shapes=[pltpu.VMEM((2,T,128),BF16)]*4+[pltpu.VMEM((2,T,128),F32)]+[pltpu.VMEM((BLK,BLK),F32)]*2),
        out_shape=[jax.ShapeDtypeStruct((3,T,HD),BF16),jax.ShapeDtypeStruct((pairs,4,2*BLK),F32)],
        name="attend_backward",
    )(sp,projected,projected,projected,grad_mixed,mixed,lse,rows)

def bias_grad(sums, buckets):
    pairs=sums.shape[0]; W=2*BLK
    tab=bucket_table(W,buckets,MAXDIST)
    assert tab[BLK]==buckets-1
    m=np.zeros((W,buckets),np.float32)
    for d in range(W):
        if tab[d]<buckets-1:
            m[d,tab[d]]=1; m[d,buckets-1]=-1
    near=sums[:,0:2].reshape(pairs*2,W); total=sums[:,2:4,0].reshape(pairs*2,1)
    last=np.zeros((1,buckets),np.float32); last[0,-1]=1
    return jnp.dot(near,jnp.asarray(m),precision=HIGHEST)+total*jnp.asarray(last)


def normalize(values):
    center = jnp.mean(values, axis=-1, keepdims=True)
    centered = values - center
    inverse = lax.rsqrt(jnp.mean(centered * centered, axis=-1, keepdims=True) + EPS)
    return (centered * inverse, inverse)


def norm_back(grad_norm, normed, inverse):
    return inverse * (
        grad_norm
        - jnp.mean(grad_norm, axis=-1, keepdims=True)
        - normed * jnp.mean(grad_norm * normed, axis=-1, keepdims=True)
    )


def gelu_back(expanded, grad_active):
    pull = jax.vjp(lambda value: jax.nn.gelu(value, approximate=True), expanded)[1]
    return pull(grad_active)[0]


def dot(a, b, ca, cb):
    return lax.dot_general(a, b, (((ca,), (cb,)), ((), ())), preferred_element_type=F32)


def swap(x):
    return lax.ppermute(x, "mp", [(0, 1), (1, 0)])


def gather_rows(x, members):
    if members == 2:
        return jnp.concatenate([x, swap(x)], axis=0)
    return lax.all_gather(x, "mp", axis=0, tiled=True)


def scatter_rows(x, members):
    if members == 2:
        own = x.shape[0] // 2
        return x[:own] + swap(x[own:].astype(BF16)).astype(F32)
    return lax.psum_scatter(x.astype(BF16), "mp", scatter_dimension=0, tiled=True).astype(F32)


def per_device(
    tokens,
    lengths,
    first_gain,
    first_shift,
    heads_weight,
    relative_bias,
    mixer_weight,
    second_gain,
    second_shift,
    expand_weight,
    expand_bias,
    reduce_weight,
    reduce_bias,
    cotangent,
):
    members = lax.axis_size("mp")
    member = lax.axis_index("mp")
    length = lengths[0]
    own = tokens.shape[0]
    whole = own * members
    buckets = relative_bias.shape[1]
    turn = member * own if members == 2 else 0
    sp = jnp.stack([jnp.asarray(turn, jnp.int32), length.astype(jnp.int32)])
    places = member * own + jnp.arange(own)
    if members == 2:
        places_all = (jnp.arange(whole) + member * own) % whole
    else:
        places_all = jnp.arange(whole)
    rows = bias_rows(relative_bias)

    source_all = gather_rows(tokens, members)
    first_norm_all, first_inverse_all = normalize(source_all.astype(F32))
    first_all = (first_norm_all * first_gain + first_shift).astype(BF16)
    projected = jnp.einsum(
        "td,cde->cte", first_all, heads_weight, preferred_element_type=F32
    ).astype(BF16)
    mixed_low, logsum = attend_forward(sp, projected, rows)
    target_all = gather_rows(cotangent, members)
    target_all = jnp.where((places_all < length)[:, None], target_all, jnp.zeros_like(target_all))
    source = tokens.astype(F32)
    attended = scatter_rows(dot(mixed_low, mixer_weight, 1, 0), members)
    middle = source + attended
    second_norm, second_inverse = normalize(middle)
    second_low = (second_norm * second_gain + second_shift).astype(BF16)
    second_all = gather_rows(second_low, members)
    expanded = dot(second_all, expand_weight, 1, 0) + expand_bias
    active_low = jax.nn.gelu(expanded, approximate=True).astype(BF16)
    grad_active = dot(target_all, reduce_weight, 1, 1)
    grad_expanded = gelu_back(expanded, grad_active).astype(BF16)
    grad_second = scatter_rows(dot(grad_expanded, expand_weight, 1, 1), members)
    reduced = scatter_rows(dot(active_low, reduce_weight, 1, 0), members)
    reduce_grad = dot(active_low, target_all, 0, 0)
    expand_grad = dot(second_all, grad_expanded, 0, 0)
    expand_bias_grad = jnp.sum(grad_expanded.astype(F32), axis=0)
    block_out = (middle + reduced + reduce_bias).astype(BF16)
    target_wide = jnp.where((places < length)[:, None], cotangent, jnp.zeros_like(cotangent)).astype(F32)
    grad_middle = target_wide + norm_back(grad_second * second_gain, second_norm, second_inverse)
    attended_all = gather_rows(grad_middle.astype(BF16), members)
    mixer_grad = dot(mixed_low, attended_all, 0, 0)
    grad_mixed = dot(attended_all, mixer_weight, 1, 1).astype(BF16)
    grad_projected, sums = attend_backward(sp, projected, grad_mixed, mixed_low, logsum, rows)
    bias_part = bias_grad(sums, buckets)
    heads_grad = jnp.einsum("td,cte->cde", first_all, grad_projected, preferred_element_type=F32)
    grad_first = scatter_rows(
        jnp.einsum("cte,cde->td", grad_projected, heads_weight, preferred_element_type=F32), members
    )
    first_norm, first_inverse = normalize(source)
    tokens_grad = (
        grad_middle + norm_back(grad_first * first_gain, first_norm, first_inverse)
    ).astype(BF16)
    first_gain_grad, first_shift_grad, second_gain_grad, second_shift_grad, reduce_bias_grad = (
        lax.psum(
            (
                jnp.sum(grad_first * first_norm, axis=0),
                jnp.sum(grad_first, axis=0),
                jnp.sum(grad_second * second_norm, axis=0),
                jnp.sum(grad_second, axis=0),
                jnp.sum(target_wide, axis=0),
            ),
            ("dp", "mp"),
        )
    )
    heads_grad, bias_part, mixer_grad, expand_grad, expand_bias_grad, reduce_grad = (
        lax.psum(heads_grad.astype(BF16), "dp").astype(F32),
        lax.psum(bias_part.astype(BF16), "dp").astype(F32),
        lax.psum(mixer_grad.astype(BF16), "dp").astype(F32),
        lax.psum(expand_grad.astype(BF16), "dp").astype(F32),
        lax.psum(expand_bias_grad.astype(BF16), "dp").astype(F32),
        lax.psum(reduce_grad.astype(BF16), "dp").astype(F32),
    )
    return (
        block_out,
        tokens_grad,
        first_gain_grad,
        first_shift_grad,
        heads_grad,
        bias_part,
        mixer_grad,
        second_gain_grad,
        second_shift_grad,
        expand_grad,
        expand_bias_grad,
        reduce_grad,
        reduce_bias_grad,
    )


def solution(mesh):
    return jax.shard_map(
        per_device,
        mesh=mesh,
        in_specs=(
            P(("dp", "mp"), None),
            P("dp"),
            P(),
            P(),
            P(None, None, "mp"),
            P("mp", None),
            P("mp", None),
            P(),
            P(),
            P(None, "mp"),
            P("mp"),
            P("mp", None),
            P(),
            P(("dp", "mp"), None),
        ),
        out_specs=(
            P(("dp", "mp"), None),
            P(("dp", "mp"), None),
            P(),
            P(),
            P(None, None, "mp"),
            P("mp", None),
            P("mp", None),
            P(),
            P(),
            P(None, "mp"),
            P("mp"),
            P("mp", None),
            P(),
        ),
        check_vma=False,
    )
```

profile of v0, /device:TPU:25, one launch (start us, length us, event | category | flops | bytes accessed | tf_op | source)
XLA Modules:
  0.0 526.1 jit_solution(4985466663083401547)
XLA Ops:
  7.2 0.0 copy-start
  7.2 0.0 all-reduce.5.cloned.1.call-start
  7.3 1.3 collective-permute-start
  9.2 0.9 slice_reduce_fusion.1
  10.1 1.2 convolution_add_fusion
  11.3 0.7 reshape.112.b_ref
  12.0 0.6 pad_add_fusion.sp
  12.6 19.1 %collective-permute-done = bf16[512,1024]{1,0:T(8,128)(2,1)} collective-permute-done((bf16[512,1024]{1,0:T(8,128)(2,1)}, bf16[512,1024]{1,0:T(8,128)(2,1)}, u32[]{:S(2)}, u32[]{:S(2)}) %collective-permute-start) | collective-permute-done | bytes 1048608 | tf_op jit(solution)/shard_map/ppermute | solution.py:259
  31.7 1.9 convert_reduce_fusion
  33.6 2.2 fusion.9
  35.8 6.5 %convert_bitcast_fusion.1.q_ref.k_ref.v_ref = bf16[3,1024,512]{2,1,0:T(8,128)(2,1)} fusion(bf16[3,1024,512]{2,1,0:T(8,128)(2,1)S(1)} %copy-done, f32[1024]{0:T(1024)S(1)} %copy-done.21, f32[1024]{0:T(1024)S(1)} %copy-done.10, f32[1024]{0:T(1024)S(1)} %add_rsqrt_fusion, f32[1024]{0:T(1024)S(1)} %broadcast_multiply_fusion, ...), kind=kOutput, calls=%fused_computation.21 | convolution fusion | flops 3232235520 | bytes 8404992 | tf_op jit(solution)/shard_map/td,cde->cte/dot_general | solution.py:309
  42.3 18.0 %attend_forward.1 = (bf16[1024,512]{1,0:T(8,128)(2,1)}, f32[4,1024,128]{2,1,0:T(8,128)}) custom-call(s32[2]{0:T(128)} %pad_add_fusion.sp, bf16[3,1024,512]{2,1,0:T(8,128)(2,1)} %convert_bitcast_fusion.1.q_ref.k_ref.v_ref, bf16[3,1024,512]{2,1,0:T(8,128)(2,1)} %convert_bitcast_fusion.1.q_ref.k_ref.v_ref, ...), custom_call_target="tpu_custom_call" | custom-call | tf_op jit(solution)/shard_map/attend_forward/pallas_call | solution.py:108
  60.3 2.9 fusion.57
  63.2 0.2 slice.97
  63.3 1.3 collective-permute-start.1
  64.6 0.2 convert_reduce_fusion.1
  64.9 21.7 %collective-permute-done.1 = bf16[512,1024]{1,0:T(8,128)(2,1)S(1)} collective-permute-done((bf16[512,1024]{1,0:T(8,128)(2,1)S(1)}, bf16[512,1024]{1,0:T(8,128)(2,1)S(1)}, u32[]{:S(2)}, u32[]{:S(2)}) %collective-permute-start.1) | collective-permute-done | bytes 1048608 | tf_op jit(solution)/shard_map/ppermute | solution.py:259
  86.5 0.7 fusion.55
  87.3 0.3 multiply_reduce_fusion.2
  87.7 0.4 add_convert_fusion
  88.1 1.3 collective-permute-start.2
  89.4 0.3 collective-permute-start.4
  89.7 20.6 %collective-permute-done.2 = bf16[512,1024]{1,0:T(8,128)(2,1)S(1)} collective-permute-done((bf16[512,1024]{1,0:T(8,128)(2,1)S(1)}, bf16[512,1024]{1,0:T(8,128)(2,1)S(1)}, u32[]{:S(2)}, u32[]{:S(2)}) %collective-permute-start.2) | collective-permute-done | bytes 1048608 | tf_op jit(solution)/shard_map/ppermute | solution.py:259
  110.3 7.6 %fusion.29 = f32[1024,2048]{1,0:T(8,128)} fusion(bf16[1024,2048]{1,0:T(8,128)(2,1)S(1)} %copy-done.16, bf16[512,1024]{1,0:T(8,128)(2,1)S(1)} %collective-permute-done.2, bf16[512,1024]{1,0:T(8,128)(2,1)S(1)} %add_convert_fusion), kind=kOutput, calls=%fused_computation.66 | convolution fusion | flops 4299161600 | bytes 14680064 | tf_op jit(solution)/shard_map/dot_general | solution.py:255
  118.0 14.8 %collective-permute-done.4 = bf16[512,1024]{1,0:T(8,128)(2,1)S(1)} collective-permute-done((bf16[512,1024]{1,0:T(8,128)(2,1)S(1)}, bf16[512,1024]{1,0:T(8,128)(2,1)S(1)}, u32[]{:S(2)}, u32[]{:S(2)}) %collective-permute-start.4) | collective-permute-done | bytes 1048608 | tf_op jit(solution)/shard_map/ppermute | solution.py:259
  132.8 14.3 %fusion.56 = (bf16[2048]{0:T(1024)(128)(2,1)S(1)}, bf16[1024,2048]{1,0:T(8,128)(2,1)}) fusion(f32[1024,2048]{1,0:T(8,128)} %fusion.29, f32[2048]{0:T(1024)S(1)} %convert_element_type.102, bf16[2048,1024]{1,0:T(8,128)(2,1)S(1)} %copy-done.17, bf16[512,1024]{1,0:T(8,128)(2,1)S(1)} %collective-permute-done.4, bf16[512,1024]{1,0:T(8,128)(2,1)S(1)} %copy-done.6, ...), kind=kOutput, calls=%fused_computation.110 | convolution fusion | flops 4346345472 | bytes 18887680 | tf_op jit(solution)/shard_map/dot_general | solution.py:255
  147.1 6.6 %fusion.58 = f32[1024,1024]{1,0:T(8,128)S(1)} fusion(bf16[1024,2048]{1,0:T(8,128)(2,1)} %get-tuple-element.74, bf16[1024,2048]{1,0:T(8,128)(2,1)S(1)} %copy-done.16), kind=kOutput, calls=%fused_computation.112 | convolution fusion | flops 4294967296 | bytes 12582912 | tf_op jit(solution)/shard_map/dot_general | solution.py:255
  153.7 0.2 slice.95
  153.9 1.3 collective-permute-start.5
  155.2 8.0 %fusion.53 = f32[1024,1024]{1,0:T(8,128)S(1)} fusion(bf16[2048,1024]{1,0:T(8,128)(2,1)S(1)} %copy-done.17, f32[1024,2048]{1,0:T(8,128)} %fusion.29, f32[2048]{0:T(1024)S(1)} %convert_element_type.102), kind=kOutput, calls=%fused_computation.107 | convolution fusion | flops 4315938816 | bytes 16785408 | tf_op jit(solution)/shard_map/dot_general | solution.py:255
  163.1 0.2 slice.96
  163.3 0.3 collective-permute-start.3
  163.6 11.6 %collective-permute-done.5 = bf16[512,1024]{1,0:T(8,128)(2,1)S(1)} collective-permute-done((bf16[512,1024]{1,0:T(8,128)(2,1)S(1)}, bf16[512,1024]{1,0:T(8,128)(2,1)S(1)}, u32[]{:S(2)}, u32[]{:S(2)}) %collective-permute-start.5) | collective-permute-done | bytes 1048608 | tf_op jit(solution)/shard_map/ppermute | solution.py:259
  175.2 1.1 multiply_reduce_fusion
  176.3 21.4 %collective-permute-done.3 = bf16[512,1024]{1,0:T(8,128)(2,1)S(1)} collective-permute-done((bf16[512,1024]{1,0:T(8,128)(2,1)S(1)}, bf16[512,1024]{1,0:T(8,128)(2,1)S(1)}, u32[]{:S(2)}, u32[]{:S(2)}) %collective-permute-start.3) | collective-permute-done | bytes 1048608 | tf_op jit(solution)/shard_map/ppermute | solution.py:259
  197.7 3.2 fusion.54
  200.9 1.3 collective-permute-start.6
  202.2 8.6 %convolution_convert_fusion = bf16[2048,1024]{1,0:T(8,128)(2,1)} fusion(bf16[512,1024]{1,0:T(8,128)(2,1)S(1)} %collective-permute-done.4, bf16[512,1024]{1,0:T(8,128)(2,1)S(1)} %copy-done.6, pred[1024]{0:T(1024)(128)(4,1)S(1)} %fusion.35, f32[1024,2048]{1,0:T(8,128)S(1)} %bitcast.32, f32[2048]{0:T(1024)S(1)} %convert_element_type.102), kind=kOutput, calls=%fused_computation.18 | convolution fusion | flops 4323278848 | bytes 14689280 | tf_op jit(solution)/shard_map/dot_general | solution.py:255
  210.8 6.1 %convolution_convert_fusion.1 = bf16[1024,2048]{1,0:T(8,128)(2,1)} fusion(bf16[1024,2048]{1,0:T(8,128)(2,1)S(1)} %copy-done.22, bf16[512,1024]{1,0:T(8,128)(2,1)S(1)} %collective-permute-done.2, bf16[512,1024]{1,0:T(8,128)(2,1)S(1)} %add_convert_fusion), kind=kOutput, calls=%fused_computation.19 | convolution fusion | flops 4301258752 | bytes 10485760 | tf_op jit(solution)/shard_map/dot_general | solution.py:255
  216.9 4.4 collective-permute-done.6
  221.3 2.3 convolution_convert_fusion.3.do_ref
  223.6 24.5 %attend_backward.1 = (bf16[3,1024,512]{2,1,0:T(8,128)(2,1)}, f32[4,4,512]{2,1,0:T(4,128)}) custom-call(s32[2]{0:T(128)} %pad_add_fusion.sp, bf16[3,1024,512]{2,1,0:T(8,128)(2,1)} %convert_bitcast_fusion.1.q_ref.k_ref.v_ref, bf16[3,1024,512]{2,1,0:T(8,128)(2,1)} %convert_bitcast_fusion.1.q_ref.k_ref.v_ref, ...), custom_call_target="tpu_custom_call" | custom-call | tf_op jit(solution)/shard_map/attend_backward/pallas_call | solution.py:209
  248.1 4.2 convolution_convert_fusion.2
  252.3 6.8 %convert_bitcast_fusion = bf16[3,1024,512]{1,2,0:T(8,128)(2,1)} fusion(bf16[3,1024,512]{2,1,0:T(8,128)(2,1)S(1)} %copy-done.18, f32[1024]{0:T(1024)S(1)} %copy-done.21, f32[1024]{0:T(1024)S(1)} %copy-done.10, f32[1024]{0:T(1024)S(1)} %add_rsqrt_fusion, f32[1024]{0:T(1024)S(1)} %broadcast_multiply_fusion, bf16[512,1024]{1,0:T(8,128)(2,1)} %collective-permute-done, ...), kind=kOutput, calls=%fused_computation.20 | convolution fusion | flops 3232235520 | bytes 8404992 | tf_op jit(solution)/shard_map/td,cte->cde/dot_general | solution.py:338
  259.1 0.0 all-reduce.5.cloned.1.call-update
  259.2 0.0 copy-start.15
  259.2 5.4 %convolution_bitcast_fusion = f32[1024,1024]{1,0:T(8,128)S(1)} fusion(bf16[3,1024,512]{2,1,0:T(8,128)(2,1)} %get-tuple-element.19, bf16[3,1024,512]{2,1,0:T(8,128)(2,1)S(1)} %copy-done), kind=kOutput, calls=%fused_computation.33 | convolution fusion | flops 3221225472 | bytes 10485760 | tf_op jit(solution)/shard_map/cte,cde->td/dot_general | solution.py:340
  264.6 2.0 copy-done.4
  266.6 1.1 slice.94
  267.7 1.2 collective-permute-start.7
  268.9 0.1 slice_reduce_fusion
  269.0 0.1 mul.213
  269.2 0.2 fusion.30
  269.4 30.4 %all-reduce.1 = (bf16[8,32]{1,0:T(8,128)(2,1)S(1)}, bf16[2048]{0:T(1024)(128)(2,1)S(1)}) all-reduce(bf16[8,32]{1,0:T(8,128)(2,1)S(1)} %fusion.30, bf16[2048]{0:T(1024)(128)(2,1)S(1)} %get-tuple-element.73), channel_id=1, replica_groups=mesh['dp'=16,'mp'=2] {'dp'}, use_global_device_ids=true, to_apply=%region_15.16 | all-reduce | flops 2304 | bytes 9216 | tf_op jit(solution)/shard_map/psum | solution.py:360
  299.8 0.6 convert_element_type.117
  300.4 0.6 convert_element_type.122
  301.0 3.4 fusion.23
  304.4 46.1 %all-reduce = (f32[1024]{0:T(1024)}, f32[1024]{0:T(1024)}, f32[1024]{0:T(1024)}, f32[1024]{0:T(1024)}, f32[1024]{0:T(1024)}) all-reduce(f32[1024]{0:T(1024)S(1)} %get-tuple-element.49, f32[1024]{0:T(1024)S(1)} %get-tuple-element.54, f32[1024]{0:T(1024)S(1)} %get-tuple-element.47, ...), channel_id=1, replica_groups=mesh['dp'=16,'mp'=2] {'dp','mp'}, use_global_device_ids=true, to_apply=%region_11.12 | all-reduce | flops 5120 | bytes 40960 | tf_op jit(solution)/shard_map/psum | solution.py:347
  350.5 4.7 fusion.22
  355.2 144.4 %all-reduce.5.cloned.1.call-done = (bf16[3,1024,512]{1,2,0:T(8,128)(2,1)}, bf16[512,1024]{1,0:T(8,128)(2,1)}, bf16[1024,2048]{1,0:T(8,128)(2,1)}, bf16[2048,1024]{1,0:T(8,128)(2,1)}) async-done(((bf16[3,1024,512]{1,2,0:T(8,128)(2,1)}, bf16[512,1024]{1,0:T(8,128)(2,1)}, bf16[1024,2048]{1,0:T(8,128)(2,1)}, bf16[2048,1024]{1,0:T(8,128)(2,1)}), (bf16[3,1024,512]{1,2,0:T(8,128)(2,1)}, ...) | async-done | bytes 12582928 | tf_op jit(solution)/shard_map/psum | solution.py:359
  499.6 2.8 convert_element_type.119
  502.4 5.4 %copy.34 = f32[3,1024,512]{2,1,0:T(8,128)} copy(bf16[3,1024,512]{1,2,0:T(8,128)(2,1)} %get-tuple-element.62) | data formatting | bytes 9437184
  507.7 6.8 %convert_element_type.121 = f32[1024,2048]{1,0:T(8,128)} convert(bf16[1024,2048]{1,0:T(8,128)(2,1)} %get-tuple-element.64) | non-fusion elementwise | flops 2097152 | bytes 12582912 | tf_op jit(solution)/shard_map/convert_element_type | solution.py:362
  514.6 4.4 convert_element_type.124
  (63 shorter events, 0.2 us)
Async XLA Ops:
  7.2 28.6 %copy-start = (bf16[3,1024,512]{2,1,0:T(8,128)(2,1)S(1)}, bf16[3,1024,512]{2,1,0:T(8,128)(2,1)}, u32[]{:S(2)}) copy-start(bf16[3,1024,512]{2,1,0:T(8,128)(2,1)} %param.22) | copy-start | bytes 9437188
  7.2 28.6 %copy-start.10 = (f32[1024]{0:T(1024)S(1)}, f32[1024]{0:T(1024)}, u32[]{:S(2)}) copy-start(f32[1024]{0:T(1024)} %param.20) | copy-start | bytes 12292
  7.2 28.6 %copy-start.21 = (f32[1024]{0:T(1024)S(1)}, f32[1024]{0:T(1024)}, u32[]{:S(2)}) copy-start(f32[1024]{0:T(1024)} %param.21) | copy-start | bytes 12292
  7.2 492.4 %all-reduce.5.cloned.1.call-start = ((), (), s32[]{:S(2)}) async-start(), calls=%async_computation | async-start | bytes 25165824 | tf_op jit(solution)/shard_map/psum | solution.py:359
  7.3 24.4 %collective-permute-start = (bf16[512,1024]{1,0:T(8,128)(2,1)}, bf16[512,1024]{1,0:T(8,128)(2,1)}, u32[]{:S(2)}, u32[]{:S(2)}) collective-permute-start(bf16[512,1024]{1,0:T(8,128)(2,1)} %param.18), channel_id=1, source_target_pairs={{0,1},{1,0},{2,3},{3,2},{4,5},{5,4},{6,7},{7,6},{8,9},{9,8},{10,11... | collective-permute-start | bytes 3145736 | tf_op jit(solution)/shard_map/ppermute | solution.py:259
  12.0 23.8 %copy-start.1 = (bf16[512,1024]{1,0:T(8,128)(2,1)S(1)}, bf16[512,1024]{1,0:T(8,128)(2,1)}, u32[]{:S(2)}) copy-start(bf16[512,1024]{1,0:T(8,128)(2,1)} %param.18) | copy-start | bytes 3145732
  60.3 4.3 copy-start.2
  63.3 23.2 %collective-permute-start.1 = (bf16[512,1024]{1,0:T(8,128)(2,1)S(1)}, bf16[512,1024]{1,0:T(8,128)(2,1)S(1)}, u32[]{:S(2)}, u32[]{:S(2)}) collective-permute-start(bf16[512,1024]{1,0:T(8,128)(2,1)S(1)} %slice.97), channel_id=1, source_target_pairs={{0,1},{1,0},{2,3},{3,2},{4,5},{5,4},{6,7},{7,6},{8,9},{9,8},{10,11... | collective-permute-start | bytes 3145736 | tf_op jit(solution)/shard_map/ppermute | solution.py:259
  64.8 22.8 %copy-start.9 = (f32[1024]{0:T(1024)S(1)}, f32[1024]{0:T(1024)}, u32[]{:S(2)}) copy-start(f32[1024]{0:T(1024)} %param.25) | copy-start | bytes 12292
  64.8 22.8 %copy-start.13 = (f32[1024]{0:T(1024)S(1)}, f32[1024]{0:T(1024)}, u32[]{:S(2)}) copy-start(f32[1024]{0:T(1024)} %param.26) | copy-start | bytes 12292
  87.3 2.1 copy-start.6
  87.3 2.4 copy-start.14
  87.3 23.1 %copy-start.16 = (bf16[1024,2048]{1,0:T(8,128)(2,1)S(1)}, bf16[1024,2048]{1,0:T(8,128)(2,1)}, u32[]{:S(2)}) copy-start(bf16[1024,2048]{1,0:T(8,128)(2,1)} %param.27) | copy-start | bytes 12582916
  88.1 22.3 %collective-permute-start.2 = (bf16[512,1024]{1,0:T(8,128)(2,1)S(1)}, bf16[512,1024]{1,0:T(8,128)(2,1)S(1)}, u32[]{:S(2)}, u32[]{:S(2)}) collective-permute-start(bf16[512,1024]{1,0:T(8,128)(2,1)S(1)} %add_convert_fusion), channel_id=1, source_target_pairs={{0,1},{1,0},{2,3},{3,2},{4,5},{5,4},{6,7},{7,6},{8,9},{9,8},{10,11... | collective-permute-start | bytes 3145736 | tf_op jit(solution)/shard_map/ppermute | solution.py:259
  89.4 43.4 %collective-permute-start.4 = (bf16[512,1024]{1,0:T(8,128)(2,1)S(1)}, bf16[512,1024]{1,0:T(8,128)(2,1)S(1)}, u32[]{:S(2)}, u32[]{:S(2)}) collective-permute-start(bf16[512,1024]{1,0:T(8,128)(2,1)S(1)} %copy-done.6), channel_id=1, source_target_pairs={{0,1},{1,0},{2,3},{3,2},{4,5},{5,4},{6,7},{7,6},{8,9},{9,8},{10,11... | collective-permute-start | bytes 3145736 | tf_op jit(solution)/shard_map/ppermute | solution.py:259
  89.7 43.1 %copy-start.17 = (bf16[2048,1024]{1,0:T(8,128)(2,1)S(1)}, bf16[2048,1024]{1,0:T(8,128)(2,1)}, u32[]{:S(2)}) copy-start(bf16[2048,1024]{1,0:T(8,128)(2,1)} %param.29) | copy-start | bytes 12582916
  153.9 21.3 %collective-permute-start.5 = (bf16[512,1024]{1,0:T(8,128)(2,1)S(1)}, bf16[512,1024]{1,0:T(8,128)(2,1)S(1)}, u32[]{:S(2)}, u32[]{:S(2)}) collective-permute-start(bf16[512,1024]{1,0:T(8,128)(2,1)S(1)} %slice.95), channel_id=1, source_target_pairs={{0,1},{1,0},{2,3},{3,2},{4,5},{5,4},{6,7},{7,6},{8,9},{9,8},{10,11... | collective-permute-start | bytes 3145736 | tf_op jit(solution)/shard_map/ppermute | solution.py:259
  163.1 34.6 %copy-start.12 = (f32[1024]{0:T(1024)S(1)}, f32[1024]{0:T(1024)}, u32[]{:S(2)}) copy-start(f32[1024]{0:T(1024)} %param.30) | copy-start | bytes 12292
  163.3 34.4 %collective-permute-start.3 = (bf16[512,1024]{1,0:T(8,128)(2,1)S(1)}, bf16[512,1024]{1,0:T(8,128)(2,1)S(1)}, u32[]{:S(2)}, u32[]{:S(2)}) collective-permute-start(bf16[512,1024]{1,0:T(8,128)(2,1)S(1)} %slice.96), channel_id=1, source_target_pairs={{0,1},{1,0},{2,3},{3,2},{4,5},{5,4},{6,7},{7,6},{8,9},{9,8},{10,11... | collective-permute-start | bytes 3145736 | tf_op jit(solution)/shard_map/ppermute | solution.py:259
  175.2 27.0 %slice-start = ((s8[8388608]{0:T(1024)(128)(4,1)}), s8[4194304]{0:T(1024)(128)(4,1)S(1)}, s32[]{:S(2)}) async-start(s8[8388608]{0:T(1024)(128)(4,1)} %bitcast.31), calls=%async_computation.1 | async-start | bytes 8388608
  197.7 4.5 slice-start.1
  200.9 20.4 %copy-start.7 = (bf16[512,1024]{1,0:T(8,128)(2,1)}, bf16[512,1024]{1,0:T(8,128)(2,1)S(1)}, u32[]{:S(2)}) copy-start(bf16[512,1024]{1,0:T(8,128)(2,1)S(1)} %get-tuple-element.66) | copy-start | bytes 3145732
  200.9 9.9 %copy-start.22 = (bf16[1024,2048]{1,0:T(8,128)(2,1)S(1)}, bf16[1024,2048]{1,0:T(8,128)(2,1)}, u32[]{:S(2)}) copy-start(bf16[1024,2048]{1,0:T(8,128)(2,1)} %get-tuple-element.74) | copy-start | bytes 12582916
  200.9 20.4 %collective-permute-start.6 = (bf16[512,1024]{1,0:T(8,128)(2,1)S(1)}, bf16[512,1024]{1,0:T(8,128)(2,1)S(1)}, u32[]{:S(2)}, u32[]{:S(2)}) collective-permute-start(bf16[512,1024]{1,0:T(8,128)(2,1)S(1)} %get-tuple-element.66), channel_id=1, source_target_pairs={{0,1},{1,0},{2,3},{3,2},{4,5},{5,4},{6,7},{7,6},{8,9},{9,8},{10,11... | collective-permute-start | bytes 3145736 | tf_op jit(solution)/shard_map/ppermute | solution.py:259
  210.8 10.5 %copy-start.19 = (bf16[512,1024]{1,0:T(8,128)(2,1)S(1)}, bf16[512,1024]{1,0:T(8,128)(2,1)}, u32[]{:S(2)}) copy-start(bf16[512,1024]{1,0:T(8,128)(2,1)} %param.24) | copy-start | bytes 3145732
  221.3 2.3 copy-start.20
  248.1 4.3 copy-start.3
  248.1 4.3 copy-start.18
  259.1 9.8 %copy-start.11 = (f32[4,4,512]{2,1,0:T(4,128)S(1)}, f32[4,4,512]{2,1,0:T(4,128)}, u32[]{:S(2)}) copy-start(f32[4,4,512]{2,1,0:T(4,128)} %get-tuple-element.20) | copy-start | bytes 98308
  259.2 10.0 %copy-start.8 = (f32[512,32]{1,0:T(8,128)S(1)}, f32[512,32]{1,0:T(8,128)}, u32[]{:S(2)}) copy-start(f32[512,32]{1,0:T(8,128)} %constant.65.clone) | copy-start | bytes 196612
  259.2 10.0 %copy-start.15 = (f32[32]{0:T(128)S(1)}, f32[32]{0:T(128)}, u32[]{:S(2)}) copy-start(f32[32]{0:T(128)} %constant.69) | copy-start | bytes 388
  264.6 2.0 copy-start.4
  267.7 33.3 %collective-permute-start.7 = (bf16[512,1024]{1,0:T(8,128)(2,1)}, bf16[512,1024]{1,0:T(8,128)(2,1)}, u32[]{:S(2)}, u32[]{:S(2)}) collective-permute-start(bf16[512,1024]{1,0:T(8,128)(2,1)} %slice.94), channel_id=1, source_target_pairs={{0,1},{1,0},{2,3},{3,2},{4,5},{5,4},{6,7},{7,6},{8,9},{9,8},{10,11... | collective-permute-start | bytes 3145736 | tf_op jit(solution)/shard_map/ppermute | solution.py:259
  507.7 6.8 %copy-start.5 = (bf16[2048,1024]{1,0:T(8,128)(2,1)S(1)}, bf16[2048,1024]{1,0:T(8,128)(2,1)}, u32[]{:S(2)}) copy-start(bf16[2048,1024]{1,0:T(8,128)(2,1)} %get-tuple-element.65) | copy-start | bytes 12582916
Sparse Core Ops, SparseCore 0:
  259.3 240.2 all-reduce.4
where the time goes:
time: 533 us; the launch traced here: 526 us
  waiting for transfers between devices  258 us (48%)
  matrix products  80.7 us (15%)
  blocking collectives  76.5 us (14%)
  Pallas kernels  42.4 us (8%)
  other arithmetic  34.1 us (6%)
  between operations  15.3 us (3%)
  local copies, waits for them, and re-layouts  10.8 us (2%)
  starting transfers between devices  8.35 us (2%)
    psum x1, waiting for transfers between devices, per_device(): lax.psum(heads_grad.astype(BF16), 'dp').astype(F32)  144 us
    ppermute x8, waiting for transfers between devices, swap(): return lax.ppermute(x, 'mp', [(0, 1), (1, 0)])  114 us
    dot_general x9, matrix products, dot(): lax.dot_general(a, b, (((ca,), (cb,)), ((), ())), preferred_element_type=...  60.6 us
    psum x1, blocking collectives, per_device(): lax.psum((jnp.sum(grad_first * first_norm, axis=0), jnp.sum(grad_first, a...  46.1 us
    psum x1, blocking collectives, per_device(): lax.psum(bias_part.astype(BF16), 'dp').astype(F32)  30.4 us
    pallas_call x1, Pallas kernels, attend_backward(): pl.pallas_call(functools.partial(bwd_kernel, variant=variant), grid_spec=...  24.5 us
    pallas_call x1, Pallas kernels, attend_forward(): pl.pallas_call(fwd_kernel, grid_spec=pltpu.PrefetchScalarGridSpec(num_sca...  18 us
  transfers between devices with their start and end apart: 9, of which 8 were waited for; matrix products, arithmetic and copies ran while one was open for 10% of the time, Pallas kernels for 0%

commit v1 on v0

v1 whole, which is shorter than its diff:
```python
import functools
import math

import jax
import jax.numpy as jnp
import numpy as np
from jax import lax
from jax.experimental import pallas as pl
from jax.experimental.pallas import tpu as pltpu
from jax.sharding import PartitionSpec as P

EPS = 1e-05
DH=64; MAXDIST=128; NEG=-1e30; BLK=256
F32=jnp.float32; BF16=jnp.bfloat16
HIGHEST=lax.Precision.HIGHEST

def bucket_table(count, buckets, reach):
    exact = buckets // 2
    entries = []
    for position in range(count):
        if position < exact:
            entries.append(position)
        else:
            level = exact + int(math.log(position / exact) / math.log(reach / exact) * (buckets - exact))
            entries.append(min(buckets - 1, level))
    return np.array(entries, dtype=np.int32)

def bias_tables(buckets):
    W=2*BLK
    tab=bucket_table(W,buckets,MAXDIST)
    oh=np.zeros((buckets,4,W),np.float32); neg=np.zeros((1,4,W),np.float32)
    for y in range(W):
        x = y if y < BLK else y-W
        if x<=0 and -x<BLK: oh[tab[-x],0,y]=1
        else: neg[0,0,y]=NEG
        d=BLK-x
        if 0<=d<W: oh[tab[d],1,y]=1
        if 0<=x: oh[tab[x],2,y]=1
        else: neg[0,2,y]=NEG
        d=BLK+x
        if 0<=d<W: oh[tab[d],3,y]=1
    return oh.reshape(buckets,4*W), neg.reshape(1,4*W)

def bias_rows(relative_bias):
    heads,buckets=relative_bias.shape
    oh,neg=bias_tables(buckets)
    rel=relative_bias-relative_bias[:,buckets-1:]
    rows=jnp.dot(rel,jnp.asarray(oh),precision=HIGHEST)+jnp.asarray(neg)
    return rows.reshape(heads//2,2,4*2*BLK)

def split3(x):
    hi=x.astype(BF16); rest=x-hi.astype(F32); mid=rest.astype(BF16)
    lo=(rest-mid.astype(F32)).astype(BF16)
    return hi.astype(F32),mid.astype(F32),lo.astype(F32)

def toeplitz(row):
    wide=jnp.broadcast_to(row,(BLK,2*BLK))
    return pltpu.roll(wide,0,1,stride=1,stride_axis=0)[:,:BLK]


def fwd_kernel(sp, a_ref,c_ref,b_ref,o_ref,lse_ref,qs,ks,vs):
    half=a_ref.shape[1]; T=2*half; flip=sp[0]; length=sp[1]
    lane=lax.broadcasted_iota(jnp.int32,(1,128),1)
    W=2*BLK
    for a,ref in enumerate((a_ref,c_ref)):
        start=pl.multiple_of((a^flip)*half,half)
        dst=pl.ds(start,half)
        q=ref[0].astype(F32); k=ref[1].astype(F32); v=ref[2].astype(F32)
        pos=lax.broadcasted_iota(jnp.int32,(half,1),0)+start
        gone=jnp.where(pos<length,0.0,NEG).astype(F32)
        for h in range(2):
            mine=(lane//DH)==h
            spare=lane==(DH*(1-h))
            qs[h,dst,:]=jnp.where(mine,q*DH**-0.5,jnp.where(spare,1.0,0.0)).astype(BF16)
            ks[h,dst,:]=jnp.where(mine,k,jnp.where(spare,gone,0.0)).astype(BF16)
            vs[h,dst,:]=jnp.where(mine,v,1.0).astype(BF16)
    for h in range(2):
        mine=(lane//DH)==h
        t0=toeplitz(b_ref[0,h:h+1,0:W]); t1=toeplitz(b_ref[0,h:h+1,W:2*W])
        for i in range(T//BLK):
            kc=(i+1)*BLK
            s=lax.dot_general(qs[h,i*BLK:kc,:],ks[h,:kc,:],(((1,),(1,)),((),())),preferred_element_type=F32)
            parts=[]
            if i>=2: parts.append(s[:,:kc-2*BLK])
            if i>=1: parts.append(s[:,kc-2*BLK:kc-BLK]+t1)
            parts.append(s[:,kc-BLK:]+t0)
            top=functools.reduce(jnp.maximum,[jnp.max(x,axis=1,keepdims=True) for x in parts])
            p=jnp.concatenate([jnp.exp(x-top).astype(BF16) for x in parts],axis=1)
            o=jnp.dot(p,vs[h,:kc,:],preferred_element_type=F32)
            total=o[:,DH*(1-h):DH*(1-h)+1]
            o=o/total
            lse=top+jnp.log(total)
            rows=pl.ds(pl.multiple_of((i*BLK+flip*half)%T,BLK),BLK)
            here=slice(i*BLK,kc)
            if h==0:
                o_ref[rows,:]=o.astype(BF16)
                lse_ref[0,here,:]=jnp.broadcast_to(lse,(BLK,128))
            else:
                o_ref[rows,:]=jnp.where(mine,o,o_ref[rows,:].astype(F32)).astype(BF16)
                lse_ref[0,here,:]=jnp.where(mine,lse,lse_ref[0,here,:])

def attend_forward(sp,projected0,projected1,rows):
    _,half,HD=projected0.shape; pairs=HD//128; T=2*half
    part=pl.BlockSpec((3,half,128),lambda p,s:(0,0,p))
    return pl.pallas_call(
        fwd_kernel,
        grid_spec=pltpu.PrefetchScalarGridSpec(
            num_scalar_prefetch=1,grid=(pairs,),
            in_specs=[part,part,pl.BlockSpec((1,2,rows.shape[2]),lambda p,s:(p,0,0))],
            out_specs=[pl.BlockSpec((T,128),lambda p,s:(0,p)),pl.BlockSpec((1,T,128),lambda p,s:(p,0,0))],
            scratch_shapes=[pltpu.VMEM((2,T,128),BF16)]*3),
        out_shape=[jax.ShapeDtypeStruct((T,HD),BF16),jax.ShapeDtypeStruct((pairs,T,128),F32)],
        cost_estimate=cost(8*T*T*HD,8*T*HD+512*pairs*T),
        name="attend_forward",
    )(sp,projected0,projected1,rows)

def diagonal_sums(acc, offset):
    W=2*BLK
    wide=jnp.concatenate([acc,jnp.zeros_like(acc)],axis=1)
    n=BLK
    while n>1:
        n//=2
        top=wide[:n]; bottom=wide[n:2*n]
        wide=top+pltpu.roll(bottom,W-n,1)
    return pltpu.roll(wide,offset,1) if offset else wide

def bwd_kernel(sp, a_ref,c_ref,d0_ref,d1_ref,o_ref,lse_ref,b_ref,g_ref,d_ref,qs,ks,vs,dos,dq,acc0,acc1):
    half=a_ref.shape[1]; T=2*half; flip=sp[0]; length=sp[1]
    lane=lax.broadcasted_iota(jnp.int32,(1,128),1)
    W=2*BLK
    n=T//BLK
    for a,(ref,do_ref) in enumerate(((a_ref,d0_ref),(c_ref,d1_ref))):
        start=pl.multiple_of((a^flip)*half,half)
        dst=pl.ds(start,half)
        q=ref[0].astype(F32); k=ref[1].astype(F32); v=ref[2].astype(F32)
        do=do_ref[...].astype(F32)
        prod=do*o_ref[a*half:(a+1)*half,:].astype(F32)
        lse=lse_ref[0,dst,:]
        pos=lax.broadcasted_iota(jnp.int32,(half,1),0)+start
        gone=jnp.where(pos<length,0.0,NEG).astype(F32)
        for h in range(2):
            mine=(lane//DH)==h
            s0=DH*(1-h)
            delta=jnp.sum(jnp.where(mine,prod,0.0),axis=1,keepdims=True)
            dh,dm,dl=split3(delta)
            lh,lm,ll=split3(lse[:,DH*h:DH*h+1])
            def lanes(base,vals):
                out=0.0
                for t,val in enumerate(vals): out=jnp.where(lane==s0+t,val,out)
                return jnp.where(mine,base,out).astype(BF16)
            qs[h,dst,:]=lanes(q*DH**-0.5,(1.0,-lh,-lm,-ll))
            ks[h,dst,:]=lanes(k,(gone,1.0,1.0,1.0))
            vs[h,dst,:]=lanes(v,(1.0,1.0,1.0))
            dos[h,dst,:]=lanes(do,(-dh,-dm,-dl))
    for h in range(2):
        mine=(lane//DH)==h
        t0=toeplitz(b_ref[0,h:h+1,2*W:3*W]); t1=toeplitz(b_ref[0,h:h+1,3*W:])
        for j in range(n):
            cols=slice(j*BLK,T)
            rj=slice(j*BLK,(j+1)*BLK)
            s=lax.dot_general(ks[h,rj,:],qs[h,cols,:],(((1,),(1,)),((),())),preferred_element_type=F32)
            dp=lax.dot_general(vs[h,rj,:],dos[h,cols,:],(((1,),(1,)),((),())),preferred_element_type=F32)
            ps=[];dss=[]
            for b in range(n-j):
                c=slice(b*BLK,(b+1)*BLK)
                x=s[:,c]
                if b==0: x=x+t0
                if b==1: x=x+t1
                p=jnp.exp(x)
                ds=p*dp[:,c]
                if b==0:
                    if j==0: acc0[...]=ds
                    else: acc0[...]+=ds
                if b==1:
                    if j==0: acc1[...]=ds
                    else: acc1[...]+=ds
                ps.append(p.astype(BF16)); dss.append(ds.astype(BF16))
            p=jnp.concatenate(ps,axis=1); ds=jnp.concatenate(dss,axis=1)
            dv=jnp.dot(p,dos[h,cols,:],preferred_element_type=F32)
            dk=jnp.dot(ds,qs[h,cols,:],preferred_element_type=F32)
            kk=jnp.where(mine,ks[h,rj,:].astype(F32),1.0).astype(BF16)
            dqj=lax.dot_general(ds,kk,(((0,),(0,)),((),())),preferred_element_type=F32)
            if j==0: dq[h,:,:]=dqj
            else: dq[h,cols,:]+=dqj
            rows=pl.ds(pl.multiple_of((j*BLK+flip*half)%T,BLK),BLK)
            if h==0:
                g_ref[1,rows,:]=dk.astype(BF16); g_ref[2,rows,:]=dv.astype(BF16)
            else:
                g_ref[1,rows,:]=jnp.where(mine,dk,g_ref[1,rows,:].astype(F32)).astype(BF16)
                g_ref[2,rows,:]=jnp.where(mine,dv,g_ref[2,rows,:].astype(F32)).astype(BF16)
        near=diagonal_sums(acc0[...],0)
        near1=diagonal_sums(acc1[...],BLK)
        d_ref[0,h:h+1,:]=near+near1
        total=jnp.sum(dq[h,:,:],axis=0,keepdims=True)[:,DH*(1-h):DH*(1-h)+1]
        d_ref[0,2+h:3+h,:]=jnp.broadcast_to(total,(1,W))
    first=(lane//DH)==0
    for a in range(2):
        dst=pl.ds(pl.multiple_of((a^flip)*half,half),half)
        g_ref[0,a*half:(a+1)*half,:]=(jnp.where(first,dq[0,dst,:],dq[1,dst,:])*DH**-0.5).astype(BF16)

def attend_backward(sp,projected0,projected1,grad0,grad1,mixed,lse,rows):
    _,half,HD=projected0.shape; pairs=HD//128; T=2*half
    part=pl.BlockSpec((3,half,128),lambda p,s:(0,0,p))
    grad=pl.BlockSpec((half,128),lambda p,s:(0,p))
    return pl.pallas_call(
        bwd_kernel,
        grid_spec=pltpu.PrefetchScalarGridSpec(
            num_scalar_prefetch=1,grid=(pairs,),
            in_specs=[part,part,grad,grad,pl.BlockSpec((T,128),lambda p,s:(0,p)),
              pl.BlockSpec((1,T,128),lambda p,s:(p,0,0)),pl.BlockSpec((1,2,rows.shape[2]),lambda p,s:(p,0,0))],
            out_specs=[pl.BlockSpec((3,T,128),lambda p,s:(0,0,p)),pl.BlockSpec((1,4,2*BLK),lambda p,s:(p,0,0))],
            scratch_shapes=[pltpu.VMEM((2,T,128),BF16)]*4+[pltpu.VMEM((2,T,128),F32)]+[pltpu.VMEM((BLK,BLK),F32)]*2),
        out_shape=[jax.ShapeDtypeStruct((3,T,HD),BF16),jax.ShapeDtypeStruct((pairs,4,2*BLK),F32)],
        cost_estimate=cost(20*T*T*HD,16*T*HD+512*pairs*T),
        name="attend_backward",
    )(sp,projected0,projected1,grad0,grad1,mixed,lse,rows)

def bias_grad(sums, buckets):
    pairs=sums.shape[0]; W=2*BLK
    tab=bucket_table(W,buckets,MAXDIST)
    assert tab[BLK]==buckets-1
    m=np.zeros((W,buckets),np.float32)
    for d in range(W):
        if tab[d]<buckets-1:
            m[d,tab[d]]=1; m[d,buckets-1]=-1
    near=sums[:,0:2].reshape(pairs*2,W); total=sums[:,2:4,0].reshape(pairs*2,1)
    last=np.zeros((1,buckets),np.float32); last[0,-1]=1
    return jnp.dot(near,jnp.asarray(m),precision=HIGHEST)+total*jnp.asarray(last)


HALF_TANH = math.sqrt(2.0 / math.pi)


def dot(a, b, ca, cb):
    return lax.dot_general(a, b, (((ca,), (cb,)), ((), ())), preferred_element_type=F32)


def fixed(shape):
    return pl.BlockSpec(shape, lambda *_: (0,) * len(shape))


def cost(flops, moved):
    return pl.CostEstimate(flops=int(flops), transcendentals=0, bytes_accessed=int(moved))


def row_norm(values):
    center = jnp.mean(values, axis=-1, keepdims=True)
    centered = values - center
    inverse = lax.rsqrt(jnp.mean(centered * centered, axis=-1, keepdims=True) + EPS)
    return centered * inverse, inverse


def project_kernel(x_ref, gain_ref, shift_ref, w_ref, low_ref, out_ref):
    normed, _ = row_norm(x_ref[...].astype(F32))
    low = (normed * gain_ref[...] + shift_ref[...]).astype(BF16)
    low_ref[...] = low
    for c in range(3):
        out_ref[c] = dot(low, w_ref[c], 1, 0).astype(BF16)


def project(x, gain, shift, weight):
    rows, model = x.shape
    width = weight.shape[2]
    step = min(256, rows)
    return pl.pallas_call(
        project_kernel,
        grid=(rows // step,),
        in_specs=[pl.BlockSpec((step, model), lambda i: (i, 0)), fixed((1, model)), fixed((1, model)), fixed(weight.shape)],
        out_specs=[pl.BlockSpec((step, model), lambda i: (i, 0)), pl.BlockSpec((3, step, width), lambda i: (0, i, 0))],
        out_shape=[jax.ShapeDtypeStruct((rows, model), BF16), jax.ShapeDtypeStruct((3, rows, width), BF16)],
        cost_estimate=cost(6 * rows * model * width, 2 * (2 * rows * model + weight.size + 3 * rows * width)),
        name="project",
    )(x, gain, shift, weight)


def mix_kernel(own_blocks, x0_ref, x1_ref, m_ref, p_ref, w0_ref, w1_ref, gain_ref, shift_ref, mid_ref, low_ref):
    i = pl.program_id(0)
    attended = dot(m_ref[...], w0_ref[...], 1, 0) + dot(p_ref[...], w1_ref[...], 1, 0)

    def rows(x_ref):
        return x_ref[...].astype(F32) + attended

    def rest(middle):
        normed, _ = row_norm(middle)
        low_ref[...] = (normed * gain_ref[...] + shift_ref[...]).astype(BF16)

    @pl.when(i < own_blocks)
    def _():
        middle = rows(x0_ref)
        mid_ref[...] = middle
        rest(middle)

    @pl.when(i >= own_blocks)
    def _():
        rest(rows(x1_ref))


def mix(tokens, other, mixed, mixed_other, weight, weight_other, gain, shift):
    own, model = tokens.shape
    width = mixed.shape[1]
    step = 256
    n = own // step
    return pl.pallas_call(
        functools.partial(mix_kernel, n),
        grid=(2 * n,),
        in_specs=[
            pl.BlockSpec((step, model), lambda i: (jnp.minimum(i, n - 1), 0)),
            pl.BlockSpec((step, model), lambda i: (jnp.maximum(i - n, 0), 0)),
            pl.BlockSpec((step, width), lambda i: (i, 0)),
            pl.BlockSpec((step, width), lambda i: ((i + n) % (2 * n), 0)),
            fixed(weight.shape), fixed(weight.shape), fixed((1, model)), fixed((1, model)),
        ],
        out_specs=[
            pl.BlockSpec((step, model), lambda i: (jnp.minimum(i, n - 1), 0)),
            pl.BlockSpec((step, model), lambda i: (i, 0)),
        ],
        out_shape=[jax.ShapeDtypeStruct((own, model), F32), jax.ShapeDtypeStruct((2 * own, model), BF16)],
        cost_estimate=cost(8 * own * model * width, 2 * (4 * own * model + 4 * own * width + 2 * weight.size) + 4 * own * model),
        name="mix",
    )(tokens, other, mixed, mixed_other, weight, weight_other, gain, shift)


def expand_kernel(x_ref, g_ref, w_ref, b_ref, act_ref, ge_ref, gs_ref, bias_ref, acc_ref):
    i = pl.program_id(0)
    x = x_ref[...]
    width = w_ref.shape[1]
    sub = 256
    total = None
    for s in range(width // sub):
        cols = slice(s * sub, (s + 1) * sub)
        u = dot(x, w_ref[:, cols], 1, 0) + b_ref[:, cols].astype(F32)
        square = u * u
        t = jnp.tanh(HALF_TANH * u * (1.0 + 0.044715 * square))
        half = 0.5 + 0.5 * t
        act_ref[:, cols] = (u * half).astype(BF16)
        slope = half + 0.5 * u * (1.0 - t * t) * (HALF_TANH * (1.0 + 3 * 0.044715 * square))
        grad = g_ref[:, cols].astype(F32) * slope
        low = grad.astype(BF16)
        ge_ref[:, cols] = low
        bias_ref[:, cols] = jnp.sum(grad, axis=0, keepdims=True)
        part = dot(low, w_ref[:, cols], 1, 1)
        total = part if total is None else total + part

    @pl.when(i == 0)
    def _():
        acc_ref[...] = total

    @pl.when(i > 0)
    def _():
        acc_ref[...] += total

    @pl.when(i == pl.num_programs(0) - 1)
    def _():
        gs_ref[...] = acc_ref[...].astype(gs_ref.dtype)


def expand(x, block, rows, grad_active, weight, bias, dtype):
    model = x.shape[1]
    hidden = weight.shape[1]
    step = min(512, hidden)
    return pl.pallas_call(
        expand_kernel,
        grid=(hidden // step,),
        in_specs=[
            pl.BlockSpec((rows, model), lambda i: (block, 0)),
            pl.BlockSpec((rows, step), lambda i: (0, i)),
            pl.BlockSpec((model, step), lambda i: (0, i)),
            pl.BlockSpec((1, step), lambda i: (0, i)),
        ],
        out_specs=[
            pl.BlockSpec((rows, step), lambda i: (0, i)),
            pl.BlockSpec((rows, step), lambda i: (0, i)),
            fixed((rows, model)),
            pl.BlockSpec((1, step), lambda i: (0, i)),
        ],
        out_shape=[
            jax.ShapeDtypeStruct((rows, hidden), BF16),
            jax.ShapeDtypeStruct((rows, hidden), BF16),
            jax.ShapeDtypeStruct((rows, model), dtype),
            jax.ShapeDtypeStruct((1, hidden), F32),
        ],
        scratch_shapes=[pltpu.VMEM((rows, model), F32)],
        cost_estimate=cost(4 * rows * model * hidden, 2 * (2 * rows * model + 3 * rows * hidden + weight.size)),
        name="expand",
    )(x, grad_active, weight, bias)


STAGES = ((1, 2, 4, 8), (1, 4, 8, 2))


def place_of(index, stages):
    bit = [(index // s) % 2 for s in stages]
    return bit[0] * 4 + bit[1] * 2 + bit[2]


def trade(x, bit):
    size = lax.axis_size("dp")
    return lax.ppermute(x, "dp", [(i, i ^ bit) for i in range(size)])


def add_low(a, b):
    return (a.astype(F32) + b.astype(F32)).astype(BF16)


def chunk_specs(tail):
    zeros = (0,) * len(tail)
    return [
        pl.BlockSpec((1, *tail), lambda g, s: (jnp.minimum(g, 3), *zeros)),
        pl.BlockSpec((1, *tail), lambda g, s: (jnp.maximum(g - 4, 0), *zeros)),
    ]


def chunk_at(slot):
    return lambda g, s: ((g + 4) % 8) ^ s[slot]


def store_chunk(value, slot, send_ref, keep_ref):
    g = pl.program_id(0)

    @pl.when(g < 4)
    def _():
        send_ref[(0, *slot)] = value

    @pl.when(g >= 4)
    def _():
        keep_ref[(0, *slot)] = value


def chunk_shapes(tail):
    return [jax.ShapeDtypeStruct((4, *tail), BF16)] * 2


def reduce_grad_kernel(s_ref, a0_ref, a1_ref, t0_ref, t1_ref, send_ref, keep_ref):
    value = dot(a0_ref[...], t0_ref[...], 0, 0) + dot(a1_ref[...], t1_ref[...], 0, 0)
    store_chunk(value.astype(BF16), (), send_ref, keep_ref)


def reduce_grad_chunks(places, slot, act0, act1, t0, t1):
    rows, hidden = act0.shape
    model = t0.shape[1]
    width = hidden // 8
    at = chunk_at(slot)
    block = pl.BlockSpec((rows, width), lambda g, s: (0, at(g, s)))
    whole = pl.BlockSpec((rows, model), lambda g, s: (0, 0))
    return pl.pallas_call(
        reduce_grad_kernel,
        grid_spec=pltpu.PrefetchScalarGridSpec(
            num_scalar_prefetch=1, grid=(8,), in_specs=[block, block, whole, whole], out_specs=chunk_specs((width, model)),
        ),
        out_shape=chunk_shapes((width, model)),
        cost_estimate=cost(4 * rows * model * hidden, 4 * rows * (model + hidden) + 2 * model * hidden),
        name="reduce_grad",
    )(places, act0, act1, t0, t1)


def expand_grad_kernel(s_ref, x_ref, g0_ref, g1_ref, send_ref, keep_ref, turned_ref):
    rows = g0_ref.shape[0]

    @pl.when(pl.program_id(0) == 0)
    def _():
        turned_ref[...] = x_ref[...].T

    value = dot(turned_ref[:, :rows], g0_ref[...], 1, 0) + dot(turned_ref[:, rows:], g1_ref[...], 1, 0)
    store_chunk(value.astype(BF16), (), send_ref, keep_ref)


def expand_grad_chunks(places, slot, x, g0, g1):
    rows, hidden = g0.shape
    model = x.shape[1]
    width = hidden // 8
    at = chunk_at(slot)
    block = pl.BlockSpec((rows, width), lambda g, s: (0, at(g, s)))
    return pl.pallas_call(
        expand_grad_kernel,
        grid_spec=pltpu.PrefetchScalarGridSpec(
            num_scalar_prefetch=1, grid=(8,),
            in_specs=[pl.BlockSpec(x.shape, lambda g, s: (0, 0)), block, block],
            out_specs=chunk_specs((model, width)),
            scratch_shapes=[pltpu.VMEM((model, x.shape[0]), BF16)],
        ),
        out_shape=chunk_shapes((model, width)),
        cost_estimate=cost(4 * rows * model * hidden, 4 * rows * (model + hidden) + 2 * model * hidden),
        name="expand_grad",
    )(places, x, g0, g1)


def heads_grad_kernel(s_ref, l0_ref, l1_ref, g_ref, send_ref, keep_ref):
    rows = l0_ref.shape[0]
    for c in range(2):
        value = dot(l0_ref[...], g_ref[c, :rows], 0, 0) + dot(l1_ref[...], g_ref[c, rows:], 0, 0)
        store_chunk(value.astype(BF16), (c,), send_ref, keep_ref)


def heads_grad_chunks(places, slot, low0, low1, grad):
    rows, model = low0.shape
    width = grad.shape[2]
    at = chunk_at(slot)
    block = pl.BlockSpec((rows, model // 8), lambda g, s: (0, at(g, s)))
    tail = (2, model // 8, width)
    return pl.pallas_call(
        heads_grad_kernel,
        grid_spec=pltpu.PrefetchScalarGridSpec(
            num_scalar_prefetch=1, grid=(8,),
            in_specs=[block, block, pl.BlockSpec((2, 2 * rows, width), lambda g, s: (0, 0, 0))],
            out_specs=chunk_specs(tail),
        ),
        out_shape=chunk_shapes(tail),
        cost_estimate=cost(8 * rows * model * width, 4 * rows * (model + 2 * width) + 4 * model * width),
        name="heads_grad",
    )(places, low0, low1, grad)


def values_grad_kernel(s_ref, l0_ref, l1_ref, g_ref, a0_ref, a1_ref, m_ref, send_ref, keep_ref):
    rows = l0_ref.shape[0]
    value = dot(l0_ref[...], g_ref[0, :rows], 0, 0) + dot(l1_ref[...], g_ref[0, rows:], 0, 0)
    store_chunk(value.astype(BF16), (0,), send_ref, keep_ref)
    value = dot(a0_ref[...], m_ref[:rows], 0, 0) + dot(a1_ref[...], m_ref[rows:], 0, 0)
    store_chunk(value.astype(BF16), (1,), send_ref, keep_ref)


def values_grad_chunks(places, slot, low0, low1, grad, att0, att1, mixed):
    rows, model = low0.shape
    width = grad.shape[2]
    at = chunk_at(slot)
    block = pl.BlockSpec((rows, model // 8), lambda g, s: (0, at(g, s)))
    tail = (2, model // 8, width)
    return pl.pallas_call(
        values_grad_kernel,
        grid_spec=pltpu.PrefetchScalarGridSpec(
            num_scalar_prefetch=1, grid=(8,),
            in_specs=[block, block, pl.BlockSpec((1, 2 * rows, width), lambda g, s: (2, 0, 0)), block, block,
                      pl.BlockSpec((2 * rows, width), lambda g, s: (0, 0))],
            out_specs=chunk_specs(tail),
        ),
        out_shape=chunk_shapes(tail),
        cost_estimate=cost(8 * rows * model * width, 4 * rows * (2 * model + 2 * width) + 4 * model * width),
        name="values_grad",
    )(places, low0, low1, grad, att0, att1, mixed)


def sum_chunks(send, keep, stages):
    got = trade(send, stages[0])
    out, stay = add_low(keep[2:], got[2:]), add_low(keep[:2], got[:2])
    got = trade(out, stages[1])
    out, stay = add_low(stay[1:], got[1:]), add_low(stay[:1], got[:1])
    got = trade(out, stages[2])
    stay = add_low(stay, got)
    stay = add_low(stay, trade(stay, stages[3]))
    first = jnp.concatenate([stay, trade(stay, stages[2])], axis=0)
    second = trade(first, stages[1])
    return first, second, trade(first, stages[0]), trade(second, stages[0])


def spread_kernel(put, s_ref, *refs):
    g = pl.program_id(0)
    pieces, outs = refs[-4 - put.outs:-put.outs], refs[-put.outs:]
    for a in range(4):
        @pl.when(g // 2 == a)
        def _(a=a):
            put(pieces[a], outs)


def spread(places, slot, pieces, put, tail, out_specs, out_shape, given=None, name=None):
    zeros = (0,) * len(tail)
    at = lambda g, s: g ^ s[slot]
    in_specs = [
        pl.BlockSpec((1, *tail), lambda g, s, a=a: (jnp.clip(g - 2 * a, 0, 1), *zeros)) for a in range(4)
    ]
    args = list(pieces)
    aliases = {}
    if given is not None:
        in_specs.insert(0, pl.BlockSpec(memory_space=pl.ANY))
        args.insert(0, given)
        aliases = {1: 0}
    return pl.pallas_call(
        functools.partial(spread_kernel, put),
        grid_spec=pltpu.PrefetchScalarGridSpec(
            num_scalar_prefetch=1, grid=(8,), in_specs=in_specs, out_specs=[spec(at) for spec in out_specs],
        ),
        out_shape=out_shape,
        input_output_aliases=aliases,
        cost_estimate=cost(0, 6 * 8 * math.prod(tail)),
        name=name,
    )(places, *args)


def put_rows(piece, outs):
    outs[0][...] = piece[0].astype(F32)


put_rows.outs = 1


def put_values(piece, outs):
    outs[0][0] = piece[0, 0].astype(F32)
    outs[1][...] = piece[0, 1].astype(F32).T


put_values.outs = 2


def normalize(values):
    return row_norm(values)


def norm_back(grad_norm, normed, inverse):
    return inverse * (
        grad_norm
        - jnp.mean(grad_norm, axis=-1, keepdims=True)
        - normed * jnp.mean(grad_norm * normed, axis=-1, keepdims=True)
    )


def gelu_back(expanded, grad_active):
    pull = jax.vjp(lambda value: jax.nn.gelu(value, approximate=True), expanded)[1]
    return pull(grad_active)[0]


def swap(x):
    return lax.ppermute(x, "mp", [(0, 1), (1, 0)])


def keep_valid(x, places, length):
    return jnp.where((places < length)[:, None], x, jnp.zeros_like(x))


def paired(
    tokens, lengths, first_gain, first_shift, heads_weight, relative_bias, mixer_weight, second_gain,
    second_shift, expand_weight, expand_bias, reduce_weight, reduce_bias, cotangent,
):
    member = lax.axis_index("mp")
    index = lax.axis_index("dp")
    length = lengths[0]
    own, model = tokens.shape
    buckets = relative_bias.shape[1]
    width = heads_weight.shape[2]
    sp = jnp.stack([member.astype(jnp.int32), length.astype(jnp.int32)])
    chunk_place = jnp.stack([place_of(index, s).astype(jnp.int32) for s in STAGES])
    places = member * own + jnp.arange(own)
    places_other = (1 - member) * own + jnp.arange(own)
    rows = bias_rows(relative_bias)
    line = lambda v: v.reshape(1, -1)

    other = swap(tokens)
    low0, projected0 = project(tokens, line(first_gain), line(first_shift), heads_weight)
    target0 = keep_valid(cotangent, places, length)
    cotangent_late, other = lax.optimization_barrier((cotangent, other))
    mixer_late, _ = lax.optimization_barrier((mixer_weight, other))
    cotangent_other = swap(cotangent_late)
    mixer_other = swap(mixer_late)
    low1, projected1 = project(other, line(first_gain), line(first_shift), heads_weight)
    mixed, logsum = attend_forward(sp, projected0, projected1, rows)
    mixed_other = swap(mixed)
    target1 = keep_valid(cotangent_other, places_other, length)
    active_grad0 = dot(target0, reduce_weight, 1, 1).astype(BF16)
    active_grad1 = dot(target1, reduce_weight, 1, 1).astype(BF16)
    middle, second = mix(tokens, other, mixed, mixed_other, mixer_weight, mixer_other, line(second_gain), line(second_shift))
    act1, ge1, gs1, eb1 = expand(second, 1, own, active_grad1, expand_weight, line(expand_bias), BF16)
    gs_got = swap(gs1)
    act0, ge0, gs0, eb0 = expand(second, 0, own, active_grad0, expand_weight, line(expand_bias), F32)

    reduce_sums = sum_chunks(*reduce_grad_chunks(chunk_place, 0, act0, act1, target0, target1), STAGES[0])
    expand_sums = sum_chunks(*expand_grad_chunks(chunk_place, 1, second, ge0, ge1), STAGES[1])

    second_norm, second_inverse = normalize(middle)
    grad_second = gs0 + gs_got.astype(F32)
    target_wide = target0.astype(F32)
    grad_middle = target_wide + norm_back(grad_second * second_gain, second_norm, second_inverse)
    attended0 = grad_middle.astype(BF16)
    attended1 = swap(attended0)
    grad_mixed0 = dot(attended0, mixer_weight, 1, 1).astype(BF16)
    grad_mixed1 = dot(attended1, mixer_weight, 1, 1).astype(BF16)

    reduced_got = swap(dot(act1, reduce_weight, 1, 0).astype(BF16))
    block_out = (middle + dot(act0, reduce_weight, 1, 0) + reduced_got.astype(F32) + reduce_bias).astype(BF16)

    grad_projected, sums = attend_backward(sp, projected0, projected1, grad_mixed0, grad_mixed1, mixed, logsum, rows)
    first_part1 = sum(dot(grad_projected[c, own:], heads_weight[c], 1, 1) for c in range(3)).astype(BF16)
    first_got = swap(first_part1)
    query_sums = sum_chunks(*heads_grad_chunks(chunk_place, 0, low0, low1, grad_projected), STAGES[0])
    value_sums = sum_chunks(
        *values_grad_chunks(chunk_place, 1, low0, low1, grad_projected, attended0, attended1, mixed), STAGES[1]
    )
    first_part0 = sum(dot(grad_projected[c, :own], heads_weight[c], 1, 1) for c in range(3))
    grad_first = first_part0 + first_got.astype(F32)
    first_norm, first_inverse = normalize(tokens.astype(F32))
    tokens_grad = (
        grad_middle + norm_back(grad_first * first_gain, first_norm, first_inverse)
    ).astype(BF16)

    both = jnp.stack([
        jnp.sum(grad_first * first_norm, axis=0),
        jnp.sum(grad_first, axis=0),
        jnp.sum(grad_second * second_norm, axis=0),
        jnp.sum(grad_second, axis=0),
        jnp.sum(target_wide, axis=0),
    ])
    both = both + swap(both)
    hidden = expand_bias.shape[0]
    bias_part = bias_grad(sums, buckets)
    pack = jnp.concatenate([both.reshape(-1), (eb0 + eb1).reshape(-1), bias_part.reshape(-1)]).reshape(-1, 128)
    for bit in (1, 2, 4, 8):
        pack = pack + trade(pack, bit)
    pack = pack.reshape(-1)
    both = pack[: 5 * model].reshape(5, model)
    expand_bias_grad = pack[5 * model : 5 * model + hidden]
    bias_part = pack[5 * model + hidden :].reshape(relative_bias.shape)

    chunk = (hidden // 8, model)
    (reduce_grad,) = spread(
        chunk_place, 0, reduce_sums, put_rows, chunk,
        [lambda at: pl.BlockSpec(chunk, lambda g, s: (at(g, s), 0))],
        [jax.ShapeDtypeStruct(reduce_weight.shape, F32)], name="spread_reduce",
    )
    turned = (model, hidden // 8)
    (expand_grad,) = spread(
        chunk_place, 1, expand_sums, put_rows, turned,
        [lambda at: pl.BlockSpec(turned, lambda g, s: (0, at(g, s)))],
        [jax.ShapeDtypeStruct(expand_weight.shape, F32)], name="spread_expand",
    )
    piece = (2, model // 8, width)
    (heads_grad,) = spread(
        chunk_place, 0, query_sums, put_rows, piece,
        [lambda at: pl.BlockSpec(piece, lambda g, s: (0, at(g, s), 0))],
        [jax.ShapeDtypeStruct(heads_weight.shape, F32)], name="spread_queries",
    )
    heads_grad, mixer_grad = spread(
        chunk_place, 1, value_sums, put_values, piece,
        [
            lambda at: pl.BlockSpec((1, model // 8, width), lambda g, s: (2, at(g, s), 0)),
            lambda at: pl.BlockSpec((width, model // 8), lambda g, s: (0, at(g, s))),
        ],
        [jax.ShapeDtypeStruct(heads_weight.shape, F32), jax.ShapeDtypeStruct(mixer_weight.shape, F32)],
        given=heads_grad, name="spread_values",
    )
    return (
        block_out, tokens_grad, both[0], both[1], heads_grad, bias_part, mixer_grad, both[2], both[3],
        expand_grad, expand_bias_grad, reduce_grad, both[4],
    )


def gathered(
    tokens, lengths, first_gain, first_shift, heads_weight, relative_bias, mixer_weight, second_gain,
    second_shift, expand_weight, expand_bias, reduce_weight, reduce_bias, cotangent,
):
    def gather(x):
        return lax.all_gather(x, "mp", axis=0, tiled=True)

    def scatter(x):
        return lax.psum_scatter(x.astype(BF16), "mp", scatter_dimension=0, tiled=True).astype(F32)

    members = lax.axis_size("mp")
    length = lengths[0]
    own = tokens.shape[0]
    whole = own * members
    half = whole // 2
    buckets = relative_bias.shape[1]
    sp = jnp.stack([jnp.zeros((), jnp.int32), length.astype(jnp.int32)])
    places = lax.axis_index("mp") * own + jnp.arange(own)
    rows = bias_rows(relative_bias)
    source_all = gather(tokens)
    first_all, projected = project(source_all, first_gain.reshape(1, -1), first_shift.reshape(1, -1), heads_weight)
    projected0, projected1 = projected[:, :half], projected[:, half:]
    mixed, logsum = attend_forward(sp, projected0, projected1, rows)
    source = tokens.astype(F32)
    middle = source + scatter(dot(mixed, mixer_weight, 1, 0))
    second_norm, second_inverse = normalize(middle)
    second_all = gather((second_norm * second_gain + second_shift).astype(BF16))
    target = keep_valid(cotangent, places, length)
    target_wide = target.astype(F32)
    target_all = gather(target)
    expanded = dot(second_all, expand_weight, 1, 0) + expand_bias
    active_low = jax.nn.gelu(expanded, approximate=True).astype(BF16)
    grad_expanded = gelu_back(expanded, dot(target_all, reduce_weight, 1, 1)).astype(BF16)
    grad_second = scatter(dot(grad_expanded, expand_weight, 1, 1))
    reduced = scatter(dot(active_low, reduce_weight, 1, 0))
    reduce_grad = dot(active_low, target_all, 0, 0)
    expand_grad = dot(second_all, grad_expanded, 0, 0)
    expand_bias_grad = jnp.sum(grad_expanded.astype(F32), axis=0)
    block_out = (middle + reduced + reduce_bias).astype(BF16)
    grad_middle = target_wide + norm_back(grad_second * second_gain, second_norm, second_inverse)
    attended_all = gather(grad_middle.astype(BF16))
    mixer_grad = dot(mixed, attended_all, 0, 0)
    grad_mixed = dot(attended_all, mixer_weight, 1, 1).astype(BF16)
    grad_projected, sums = attend_backward(
        sp, projected0, projected1, grad_mixed[:half], grad_mixed[half:], mixed, logsum, rows
    )
    bias_part = bias_grad(sums, buckets)
    heads_grad = jnp.einsum("td,cte->cde", first_all, grad_projected, preferred_element_type=F32)
    grad_first = scatter(jnp.einsum("cte,cde->td", grad_projected, heads_weight, preferred_element_type=F32))
    first_norm, first_inverse = normalize(source)
    tokens_grad = (
        grad_middle + norm_back(grad_first * first_gain, first_norm, first_inverse)
    ).astype(BF16)
    first_gain_grad, first_shift_grad, second_gain_grad, second_shift_grad, reduce_bias_grad = (
        lax.psum(
            (
                jnp.sum(grad_first * first_norm, axis=0),
                jnp.sum(grad_first, axis=0),
                jnp.sum(grad_second * second_norm, axis=0),
                jnp.sum(grad_second, axis=0),
                jnp.sum(target_wide, axis=0),
            ),
            ("dp", "mp"),
        )
    )
    heads_grad, bias_part, mixer_grad, expand_grad, expand_bias_grad, reduce_grad = (
        lax.psum(x.astype(BF16), "dp").astype(F32)
        for x in (heads_grad, bias_part, mixer_grad, expand_grad, expand_bias_grad, reduce_grad)
    )
    return (
        block_out, tokens_grad, first_gain_grad, first_shift_grad, heads_grad, bias_part, mixer_grad,
        second_gain_grad, second_shift_grad, expand_grad, expand_bias_grad, reduce_grad, reduce_bias_grad,
    )


def per_device(*args):
    if lax.axis_size("mp") == 2 and lax.axis_size("dp") == 16:
        return paired(*args)
    return gathered(*args)


def solution(mesh):
    return jax.shard_map(
        per_device,
        mesh=mesh,
        in_specs=(
            P(("dp", "mp"), None),
            P("dp"),
            P(),
            P(),
            P(None, None, "mp"),
            P("mp", None),
            P("mp", None),
            P(),
            P(),
            P(None, "mp"),
            P("mp"),
            P("mp", None),
            P(),
            P(("dp", "mp"), None),
        ),
        out_specs=(
            P(("dp", "mp"), None),
            P(("dp", "mp"), None),
            P(),
            P(),
            P(None, None, "mp"),
            P("mp", None),
            P("mp", None),
            P(),
            P(),
            P(None, "mp"),
            P("mp"),
            P("mp", None),
            P(),
        ),
        check_vma=False,
    )
```

time: 533 us -> 515 us (0.966)
  Pallas kernels: 42.4 us -> 168 us
  blocking collectives: 76.5 us -> 0 us
  waiting for transfers between devices: 258 us -> 207 us
  matrix products: 80.7 us -> 43 us
  starting transfers between devices: 8.35 us -> 37.6 us
  between operations: 15.3 us -> 2.21 us
    psum x1 -> x0, waiting for transfers between devices: 144 us -> none  [per_device(): lax.psum(heads_grad.astype(BF16), 'dp').astype(F32)]
    ppermute x0 -> x36, waiting for transfers between devices: none -> 135 us  [trade(): return lax.ppermute(x, 'dp', [(i, i ^ bit) for i in range(size)])]
    pallas_call x1 -> x14, Pallas kernels: 24.5 us -> 148 us  [the longest x4 31.5 us: spread(): pl.pallas_call(functools.partial(spread_kernel, put), grid_spec=pltpu.Pre...]
    psum x2 -> x0, blocking collectives: 76.5 us -> none  [the longest x1 46.1 us: per_device(): lax.psum((jnp.sum(grad_first * first_norm, axis=0), jnp.sum(grad_first, a...]
    ppermute x8 -> x9, waiting for transfers between devices: 114 us -> 71.7 us  [swap(): return lax.ppermute(x, 'mp', [(0, 1), (1, 0)])]
    ppermute x0 -> x36, starting transfers between devices: none -> 30.2 us  [trade(): return lax.ppermute(x, 'dp', [(i, i ^ bit) for i in range(size)])]
    dot_general x9 -> x12, matrix products: 60.6 us -> 41.6 us  [dot(): lax.dot_general(a, b, (((ca,), (cb,)), ((), ())), preferred_element_type=...]
    dot_general x3 -> x0, matrix products: 18.6 us -> none  [the longest x1 6.79 us: per_device(): jnp.einsum('td,cte->cde', first_all, grad_projected, preferred_element_ty...]
  transfers between devices with their start and end apart: 9 -> 45, of which waited for: 8 -> 16; matrix products, arithmetic and copies ran while one was open for 10% -> 16% of each run, Pallas kernels for 0% -> 28%
where the time goes in v1:
time: 515 us; the launch traced here: 504 us
  waiting for transfers between devices  207 us (40%)
  Pallas kernels  168 us (33%)
  matrix products  43 us (8%)
  other arithmetic  38.5 us (7%)
  starting transfers between devices  37.6 us (7%)
  local copies, waits for them, and re-layouts  8.34 us (2%)
    ppermute x36, waiting for transfers between devices, trade(): return lax.ppermute(x, 'dp', [(i, i ^ bit) for i in range(size)])  135 us
    ppermute x9, waiting for transfers between devices, swap(): return lax.ppermute(x, 'mp', [(0, 1), (1, 0)])  71.7 us
    dot_general x12, matrix products, dot(): lax.dot_general(a, b, (((ca,), (cb,)), ((), ())), preferred_element_type=...  41.6 us
    pallas_call x4, Pallas kernels, spread(): pl.pallas_call(functools.partial(spread_kernel, put), grid_spec=pltpu.Pre...  31.5 us
    ppermute x36, starting transfers between devices, trade(): return lax.ppermute(x, 'dp', [(i, i ^ bit) for i in range(size)])  30.2 us
    pallas_call x1, Pallas kernels, attend_backward(): pl.pallas_call(bwd_kernel, grid_spec=pltpu.PrefetchScalarGridSpec(num_sca...  28.8 us
    pallas_call x2, Pallas kernels, expand(): pl.pallas_call(expand_kernel, grid=(hidden // step,), in_specs=[pl.BlockS...  24.1 us
    convert_element_type x16, other arithmetic, add_low(): return (a.astype(F32) + b.astype(F32)).astype(BF16)  23.9 us
  transfers between devices with their start and end apart: 45, of which 16 were waited for; matrix products, arithmetic and copies ran while one was open for 16% of the time, Pallas kernels for 28%

profile of v1, /device:TPU:25, one launch (start us, length us, event | category | flops | bytes accessed | tf_op | source)
XLA Modules:
  0.0 504.4 jit_solution(14488836233221008481)
XLA Ops:
  0.6 1.3 collective-permute-start
  1.9 1.5 convert_reduce_fusion
  7.6 1.3 reshape.141.b_ref
  8.9 5.6 %project.2 = (bf16[512,1024]{1,0:T(8,128)(2,1)}, bf16[3,512,512]{2,1,0:T(8,128)(2,1)}) custom-call(bf16[512,1024]{1,0:T(8,128)(2,1)} %x0_ref.1, f32[1,1024]{1,0:T(1,128)} %bitcast.95, f32[1,1024]{1,0:T(1,128)} %bitcast.97, bf16[3,1024,512]{2,1,0:T(8,128)(2,1)} %w_ref.5), custom_call_target="tpu_custom_call" | custom-call | flops 1610612736 | bytes 6815744 | tf_op jit(solution)/shard_map/project/pallas_call | solution.py:265
  14.8 6.3 %convolution_convert_fusion.1.g_ref = bf16[512,2048]{1,0:T(8,128)(2,1)} fusion(bf16[512,1024]{1,0:T(8,128)(2,1)S(1)} %get-tuple-element.84.t0_ref, bf16[2048,1024]{1,0:T(8,128)(2,1)} %param.29), kind=kOutput, calls=%fused_computation.1 | convolution fusion | flops 2148532224 | bytes 7340032 | tf_op jit(solution)/shard_map/dot_general | solution.py:235
  21.1 3.8 collective-permute-done.x_ref.x1_ref
  27.3 5.5 %project.3 = (bf16[512,1024]{1,0:T(8,128)(2,1)}, bf16[3,512,512]{2,1,0:T(8,128)(2,1)}) custom-call(bf16[512,1024]{1,0:T(8,128)(2,1)} %copy-done.38, f32[1,1024]{1,0:T(1,128)} %bitcast.96, f32[1,1024]{1,0:T(1,128)} %bitcast.98, bf16[3,1024,512]{2,1,0:T(8,128)(2,1)} %w_ref.5), custom_call_target="tpu_custom_call" | custom-call | flops 1610612736 | bytes 6815744 | tf_op jit(solution)/shard_map/project/pallas_call | solution.py:265
  32.8 19.7 %attend_forward.1 = (bf16[1024,512]{1,0:T(8,128)(2,1)}, f32[4,1024,128]{2,1,0:T(8,128)}) custom-call(s32[2]{0:T(128)} %pad_add_fusion.sp, bf16[3,512,512]{2,1,0:T(8,128)(2,1)} %get-tuple-element.45.a_ref, bf16[3,512,512]{2,1,0:T(8,128)(2,1)} %get-tuple-element.46.c_ref, f32[4,2,2048]{2,1,0:T(2,128)} %reshape.138.b_ref), custom_call_target="tpu_custom_call" | custom-call | flops 4294967296 | bytes 6291456 | tf_op jit(solution)/shard_map/attend_forward/pallas_call | solution.py:105
  54.1 6.3 %convolution_convert_fusion.g_ref = bf16[512,2048]{1,0:T(8,128)(2,1)} fusion(bf16[512,1024]{1,0:T(8,128)(2,1)S(1)} %broadcast_select_fusion.t1_ref, bf16[2048,1024]{1,0:T(8,128)(2,1)} %param.29), kind=kOutput, calls=%fused_computation | convolution fusion | flops 2148532224 | bytes 7340032 | tf_op jit(solution)/shard_map/dot_general | solution.py:235
  60.4 15.1 %collective-permute-done.1.p_ref = bf16[1024,512]{1,0:T(8,128)(2,1)S(1)} collective-permute-done((bf16[1024,512]{1,0:T(8,128)(2,1)}, bf16[1024,512]{1,0:T(8,128)(2,1)S(1)}, u32[]{:S(2)}, u32[]{:S(2)}) %collective-permute-start.1) | collective-permute-done | bytes 1048608 | tf_op jit(solution)/shard_map/ppermute | solution.py:620
  75.5 22.5 %collective-permute-done.2.w1_ref = bf16[512,1024]{1,0:T(8,128)(2,1)S(1)} collective-permute-done((bf16[512,1024]{1,0:T(8,128)(2,1)S(1)}, bf16[512,1024]{1,0:T(8,128)(2,1)S(1)}, u32[]{:S(2)}, u32[]{:S(2)}) %collective-permute-start.2) | collective-permute-done | bytes 1048608 | tf_op jit(solution)/shard_map/ppermute | solution.py:620
  99.0 8.3 %mix.1 = (f32[512,1024]{1,0:T(8,128)}, bf16[1024,1024]{1,0:T(8,128)(2,1)}) custom-call(bf16[512,1024]{1,0:T(8,128)(2,1)} %x0_ref.1, bf16[512,1024]{1,0:T(8,128)(2,1)} %copy-done.38, bf16[1024,512]{1,0:T(8,128)(2,1)} %get-tuple-element.47.m_ref.o_ref, bf16[1024,512]{1,0:T(8,128)(2,1)} %copy-done.39, bf16[512,1024]{1,0:T(8,128)(2,1)} %w0_ref.1, ...), custom_call_target="tpu_custom_call" | custom-call | flops 2147483648 | bytes 10485760 | tf_op jit(solution)/shard_map/mix/pallas_call | solution.py:303
  107.3 11.8 %expand.3 = (bf16[512,2048]{1,0:T(8,128)(2,1)}, bf16[512,2048]{1,0:T(8,128)(2,1)}, bf16[512,1024]{1,0:T(8,128)(2,1)}, f32[1,2048]{1,0:T(1,128)}) custom-call(bf16[1024,1024]{1,0:T(8,128)(2,1)} %get-tuple-element.50.x_ref, bf16[512,2048]{1,0:T(8,128)(2,1)} %convolution_convert_fusion.g_ref, bf16[1024,2048]{1,0:T(8,128)(2,1)} %w_ref.7, ...), custom_call_target="tpu_custom_call" | custom-call | flops 4294967296 | bytes 12582912 | tf_op jit(solution)/shard_map/expand/pallas_call | solution.py:361
  119.1 6.3 %convolution_convert_fusion.2 = bf16[512,1024]{1,0:T(8,128)(2,1)} fusion(bf16[512,2048]{1,0:T(8,128)(2,1)} %get-tuple-element.53.a1_ref, bf16[2048,1024]{1,0:T(8,128)(2,1)} %param.29), kind=kOutput, calls=%fused_computation.33 | convolution fusion | flops 2148007936 | bytes 7340032 | tf_op jit(solution)/shard_map/dot_general | solution.py:235
  127.4 12.3 %expand.2 = (bf16[512,2048]{1,0:T(8,128)(2,1)}, bf16[512,2048]{1,0:T(8,128)(2,1)}, f32[512,1024]{1,0:T(8,128)}, f32[1,2048]{1,0:T(1,128)}) custom-call(bf16[1024,1024]{1,0:T(8,128)(2,1)} %get-tuple-element.50.x_ref, bf16[512,2048]{1,0:T(8,128)(2,1)} %convolution_convert_fusion.1.g_ref, bf16[1024,2048]{1,0:T(8,128)(2,1)} %w_ref.7, bf16[1,2048]{1,0:T(2,128)(2,1)} %reshape.141.b_ref), custom_call_target="tpu_custom_call" | custom-call | flops 4294967296 | bytes 12582912 | tf_op jit(solution)/shard_map/expand/pallas_call | solution.py:361
  139.7 30.3 %collective-permute-done.5 = bf16[512,1024]{1,0:T(8,128)(2,1)S(1)} collective-permute-done((bf16[512,1024]{1,0:T(8,128)(2,1)}, bf16[512,1024]{1,0:T(8,128)(2,1)S(1)}, u32[]{:S(2)}, u32[]{:S(2)}) %collective-permute-start.5) | collective-permute-done | bytes 1048608 | tf_op jit(solution)/shard_map/ppermute | solution.py:620
  170.0 3.0 multiply_reduce_fusion
  173.1 3.5 fusion.44
  176.9 11.8 %expand_grad.1 = (bf16[4,1024,256]{2,1,0:T(8,128)(2,1)}, bf16[4,1024,256]{2,1,0:T(8,128)(2,1)}) custom-call(s32[2]{0:T(128)} %pad_add_fusion.1.s_ref, bf16[1024,1024]{1,0:T(8,128)(2,1)} %get-tuple-element.50.x_ref, bf16[512,2048]{1,0:T(8,128)(2,1)} %get-tuple-element.69.g0_ref, bf16[512,2048]{1,0:T(8,128)(2,1)} %get-tuple-element.70.g1_ref), custom_call_target="tpu_custom_call" | custom-call | flops 4294967296 | bytes 10485760 | tf_op jit(solution)/shard_map/expand_grad/pallas_call | solution.py:473
  188.7 3.9 collective-permute-start.29
  192.6 11.7 %reduce_grad.1 = (bf16[4,256,1024]{2,1,0:T(8,128)(2,1)}, bf16[4,256,1024]{2,1,0:T(8,128)(2,1)}) custom-call(s32[2]{0:T(128)} %pad_add_fusion.1.s_ref, bf16[512,2048]{1,0:T(8,128)(2,1)} %get-tuple-element.51.a0_ref, bf16[512,2048]{1,0:T(8,128)(2,1)} %get-tuple-element.53.a1_ref, bf16[512,1024]{1,0:T(8,128)(2,1)} %copy-done.9, bf16[512,1024]{1,0:T(8,128)(2,1)} %copy-done.23), custom_call_target="tpu_custom_call" | custom-call | flops 4294967296 | bytes 10485760 | tf_op jit(solution)/shard_map/reduce_grad/pallas_call | solution.py:445
  204.4 2.8 convolution_convert_fusion.4.d0_ref
  207.3 2.8 convolution_convert_fusion.3.d1_ref
  210.0 28.8 %attend_backward.1 = (bf16[3,1024,512]{2,1,0:T(8,128)(2,1)}, f32[4,4,512]{2,1,0:T(4,128)}) custom-call(s32[2]{0:T(128)} %pad_add_fusion.sp, bf16[3,512,512]{2,1,0:T(8,128)(2,1)} %get-tuple-element.45.a_ref, bf16[3,512,512]{2,1,0:T(8,128)(2,1)} %get-tuple-element.46.c_ref, bf16[512,512]{1,0:T(8,128)(2,1)} %convolution_convert_fusion.4.d0_ref, ...), custom_call_target="tpu_custom_call" | custom-call | flops 10737418240 | bytes 10485760 | tf_op jit(solution)/shard_map/attend_backward/pallas_call | solution.py:205
  238.8 2.3 fusion.18
  241.2 1.8 fusion.14
  243.0 2.8 add_convert_fusion.4
  247.1 10.0 %heads_grad.1 = (bf16[4,2,128,512]{3,2,1,0:T(8,128)(2,1)}, bf16[4,2,128,512]{3,2,1,0:T(8,128)(2,1)}) custom-call(s32[2]{0:T(128)} %pad_add_fusion.1.s_ref, bf16[512,1024]{1,0:T(8,128)(2,1)} %get-tuple-element.61.l0_ref, bf16[512,1024]{1,0:T(8,128)(2,1)} %get-tuple-element.62.l1_ref, bf16[3,1024,512]{2,1,0:T(8,128)(2,1)} %get-tuple-element.57.g_ref), custom_call_target="tpu_custom_call" | custom-call | flops 2147483648 | bytes 6291456 | tf_op jit(solution)/shard_map/heads_grad/pallas_call | solution.py:500
  257.8 10.7 %values_grad.1 = (bf16[4,2,128,512]{3,2,1,0:T(8,128)(2,1)}, bf16[4,2,128,512]{3,2,1,0:T(8,128)(2,1)}) custom-call(s32[2]{0:T(128)} %pad_add_fusion.1.s_ref, bf16[512,1024]{1,0:T(8,128)(2,1)} %get-tuple-element.61.l0_ref, bf16[512,1024]{1,0:T(8,128)(2,1)} %get-tuple-element.62.l1_ref, bf16[3,1024,512]{2,1,0:T(8,128)(2,1)} %get-tuple-element.57.g_ref, ...), custom_call_target="tpu_custom_call" | custom-call | flops 2147483648 | bytes 8388608 | tf_op jit(solution)/shard_map/values_grad/pallas_call | solution.py:527
  268.6 4.0 add_convert_fusion.3
  273.1 4.7 add_convert_fusion.1
  279.3 1.3 collective-permute-start.38
  280.6 4.1 fusion.10
  285.1 2.8 add_convert_fusion.17
  288.3 2.5 add_convert_fusion.15
  290.8 1.3 collective-permute-start.22
  292.1 5.4 %collective-permute-done.30 = bf16[2,1024,256]{2,1,0:T(8,128)(2,1)} collective-permute-done((bf16[2,1024,256]{2,1,0:T(8,128)(2,1)}, bf16[2,1024,256]{2,1,0:T(8,128)(2,1)}, u32[]{:S(2)}, u32[]{:S(2)}) %collective-permute-start.30) | collective-permute-done | bytes 1048608 | tf_op jit(solution)/shard_map/ppermute | solution.py:398
  297.5 2.2 collective-permute-start.9
  299.8 1.4 add_convert_fusion.12
  301.3 2.3 collective-permute-done.38
  304.8 1.4 add_convert_fusion.8
  306.3 9.3 %collective-permute-done.10 = f32[58,128]{1,0:T(8,128)S(1)} collective-permute-done((f32[58,128]{1,0:T(8,128)S(1)}, f32[58,128]{1,0:T(8,128)S(1)}, u32[]{:S(2)}, u32[]{:S(2)}) %collective-permute-start.10) | collective-permute-done | bytes 29728 | tf_op jit(solution)/shard_map/ppermute | solution.py:398
  315.6 1.3 collective-permute-start.39
  318.2 1.4 collective-permute-start.15
  320.5 6.5 %collective-permute-done.31 = bf16[1,1024,256]{2,1,0:T(8,128)(2,1)S(1)} collective-permute-done((bf16[1,1024,256]{2,1,0:T(8,128)(2,1)S(1)}, bf16[1,1024,256]{2,1,0:T(8,128)(2,1)S(1)}, u32[]{:S(2)}, u32[]{:S(2)}) %collective-permute-start.31) | collective-permute-done | bytes 524320 | tf_op jit(solution)/shard_map/ppermute | solution.py:398
  328.3 11.7 %collective-permute-done.39 = bf16[1,256,1024]{2,1,0:T(8,128)(2,1)S(1)} collective-permute-done((bf16[1,256,1024]{2,1,0:T(8,128)(2,1)S(1)}, bf16[1,256,1024]{2,1,0:T(8,128)(2,1)S(1)}, u32[]{:S(2)}, u32[]{:S(2)}) %collective-permute-start.39) | collective-permute-done | bytes 524320 | tf_op jit(solution)/shard_map/ppermute | solution.py:398
  341.2 1.3 add_convert_fusion.7
  342.5 3.8 collective-permute-done.15
  347.4 2.4 collective-permute-start.16
  350.9 1.3 collective-permute-start.24
  352.3 41.5 %collective-permute-done.16 = bf16[1,2,128,512]{3,2,1,0:T(8,128)(2,1)S(1)} collective-permute-done((bf16[1,2,128,512]{3,2,1,0:T(8,128)(2,1)S(1)}, bf16[1,2,128,512]{3,2,1,0:T(8,128)(2,1)S(1)}, u32[]{:S(2)}, u32[]{:S(2)}) %collective-permute-start.16) | collective-permute-done | bytes 262176 | tf_op jit(solution)/shard_map/ppermute | solution.py:398
  394.1 1.5 collective-permute-start.41
  395.6 17.0 %collective-permute-done.17 = bf16[1,2,128,512]{3,2,1,0:T(8,128)(2,1)S(1)} collective-permute-done((bf16[1,2,128,512]{3,2,1,0:T(8,128)(2,1)S(1)}, bf16[1,2,128,512]{3,2,1,0:T(8,128)(2,1)S(1)}, u32[]{:S(2)}, u32[]{:S(2)}) %collective-permute-start.17) | collective-permute-done | bytes 262176 | tf_op jit(solution)/shard_map/ppermute | solution.py:398
  414.0 2.3 collective-permute-start.19
  417.5 6.4 %collective-permute-done.41 = bf16[1,256,1024]{2,1,0:T(8,128)(2,1)S(1)} collective-permute-done((bf16[1,256,1024]{2,1,0:T(8,128)(2,1)S(1)}, bf16[1,256,1024]{2,1,0:T(8,128)(2,1)S(1)}, u32[]{:S(2)}, u32[]{:S(2)}) %collective-permute-start.41) | collective-permute-done | bytes 524320 | tf_op jit(solution)/shard_map/ppermute | solution.py:398
  425.0 6.3 %collective-permute-done.25 = bf16[1,2,128,512]{3,2,1,0:T(8,128)(2,1)S(1)} collective-permute-done((bf16[1,2,128,512]{3,2,1,0:T(8,128)(2,1)S(1)}, bf16[1,2,128,512]{3,2,1,0:T(8,128)(2,1)S(1)}, u32[]{:S(2)}, u32[]{:S(2)}) %collective-permute-start.25) | collective-permute-done | bytes 262176 | tf_op jit(solution)/shard_map/ppermute | solution.py:398
  432.0 3.9 collective-permute-start.27
  436.0 4.7 add_convert_fusion.5
  440.8 24.5 %collective-permute-done.26.refs_2_ = bf16[2,2,128,512]{3,2,1,0:T(8,128)(2,1)} collective-permute-done((bf16[2,2,128,512]{3,2,1,0:T(8,128)(2,1)S(1)}, bf16[2,2,128,512]{3,2,1,0:T(8,128)(2,1)}, u32[]{:S(2)}, u32[]{:S(2)}) %collective-permute-start.26) | collective-permute-done | bytes 524320 | tf_op jit(solution)/shard_map/ppermute | solution.py:398
  467.0 1.7 fusion.9
  470.7 7.0 %spread_queries.1.refs_0_ = f32[3,1024,512]{2,1,0:T(8,128)} custom-call(s32[2]{0:T(128)} %pad_add_fusion.1.s_ref, bf16[2,2,128,512]{3,2,1,0:T(8,128)(2,1)} %copy-done.14, bf16[2,2,128,512]{3,2,1,0:T(8,128)(2,1)} %copy-done.24, bf16[2,2,128,512]{3,2,1,0:T(8,128)(2,1)} %copy-done.25, bf16[2,2,128,512]{3,2,1,0:T(8,128)(2,1)} %copy-done.27), custom_call_target="tpu_custom_call" | custom-call | bytes 6291456 | tf_op jit(solution)/shard_map/spread_queries/pallas_call | solution.py:575
  477.7 7.3 %spread_values.1 = (f32[3,1024,512]{2,1,0:T(8,128)}, f32[512,1024]{1,0:T(8,128)}) custom-call(s32[2]{0:T(128)} %pad_add_fusion.1.s_ref, f32[3,1024,512]{2,1,0:T(8,128)} %spread_queries.1.refs_0_, bf16[2,2,128,512]{3,2,1,0:T(8,128)(2,1)} %copy-done.15, bf16[2,2,128,512]{3,2,1,0:T(8,128)(2,1)} %collective-permute-done.26.refs_2_, ...), custom_call_target="tpu_custom_call", output_to_operand_aliasing={{0}: (1, {})} | custom-call | bytes 6291456 | tf_op jit(solution)/shard_map/spread_values/pallas_call | solution.py:575
  486.0 8.6 %spread_expand.1 = f32[1024,2048]{1,0:T(8,128)} custom-call(s32[2]{0:T(128)} %pad_add_fusion.1.s_ref, bf16[2,1024,256]{2,1,0:T(8,128)(2,1)} %pad_maximum_fusion.refs_0_, bf16[2,1024,256]{2,1,0:T(8,128)(2,1)} %collective-permute-done.34.refs_1_, bf16[2,1024,256]{2,1,0:T(8,128)(2,1)} %copy-done.21, bf16[2,1024,256]{2,1,0:T(8,128)(2,1)} %collective-permute-done.36.refs_3_), custom_call_target="tpu_custom_call" | custom-call | bytes 12582912 | tf_op jit(solution)/shard_map/spread_expand/pallas_call | solution.py:575
  495.6 8.6 %spread_reduce.1 = f32[2048,1024]{1,0:T(8,128)} custom-call(s32[2]{0:T(128)} %pad_add_fusion.1.s_ref, bf16[2,256,1024]{2,1,0:T(8,128)(2,1)} %pad_maximum_fusion.1.refs_0_, bf16[2,256,1024]{2,1,0:T(8,128)(2,1)} %collective-permute-done.42.refs_1_, bf16[2,256,1024]{2,1,0:T(8,128)(2,1)} %copy-done.20, bf16[2,256,1024]{2,1,0:T(8,128)(2,1)} %collective-permute-done.44.refs_3_), custom_call_target="tpu_custom_call" | custom-call | bytes 12582912 | tf_op jit(solution)/shard_map/spread_reduce/pallas_call | solution.py:575
  (202 shorter events, 34.9 us)
Async XLA Ops:
  0.6 24.3 %collective-permute-start = (bf16[512,1024]{1,0:T(8,128)(2,1)}, bf16[512,1024]{1,0:T(8,128)(2,1)S(1)}, u32[]{:S(2)}, u32[]{:S(2)}) collective-permute-start(bf16[512,1024]{1,0:T(8,128)(2,1)} %x0_ref.1), channel_id=1, source_target_pairs={{0,1},{1,0},{2,3},{3,2},{4,5},{5,4},{6,7},{7,6},{8,9},{9,8},{10,11... | collective-permute-start | bytes 3145736 | tf_op jit(solution)/shard_map/ppermute | solution.py:620
  14.8 12.0 %copy-start.2 = (bf16[512,1024]{1,0:T(8,128)(2,1)S(1)}, bf16[512,1024]{1,0:T(8,128)(2,1)}, u32[]{:S(2)}) copy-start(bf16[512,1024]{1,0:T(8,128)(2,1)} %x0_ref.1) | copy-start | bytes 3145732
  24.9 29.0 %collective-permute-start.3 = (bf16[512,1024]{1,0:T(8,128)(2,1)S(1)}, bf16[512,1024]{1,0:T(8,128)(2,1)S(1)}, u32[]{:S(2)}, u32[]{:S(2)}) collective-permute-start(bf16[512,1024]{1,0:T(8,128)(2,1)S(1)} %copy-done.22), channel_id=1, source_target_pairs={{0,1},{1,0},{2,3},{3,2},{4,5},{5,4},{6,7},{7,6},{8,9},{9,8},{10,11... | collective-permute-start | bytes 3145736 | tf_op jit(solution)/shard_map/ppermute | solution.py:620
  32.8 19.9 %copy-start.36 = (bf16[512,1024]{1,0:T(8,128)(2,1)S(1)}, bf16[512,1024]{1,0:T(8,128)(2,1)}, u32[]{:S(2)}) copy-start(bf16[512,1024]{1,0:T(8,128)(2,1)} %w0_ref.1) | copy-start | bytes 3145732
  52.5 23.0 %collective-permute-start.1 = (bf16[1024,512]{1,0:T(8,128)(2,1)}, bf16[1024,512]{1,0:T(8,128)(2,1)S(1)}, u32[]{:S(2)}, u32[]{:S(2)}) collective-permute-start(bf16[1024,512]{1,0:T(8,128)(2,1)} %get-tuple-element.47.m_ref.o_ref), channel_id=1, source_target_pairs={{0,1},{1,0},{2,3},{3,2},{4,5},{5,4},{6,7},{7,6},{8,9},{9,8},{10,11... | collective-permute-start | bytes 3145736 | tf_op jit(solution)/shard_map/ppermute | solution.py:620
  52.7 45.2 %collective-permute-start.2 = (bf16[512,1024]{1,0:T(8,128)(2,1)S(1)}, bf16[512,1024]{1,0:T(8,128)(2,1)S(1)}, u32[]{:S(2)}, u32[]{:S(2)}) collective-permute-start(bf16[512,1024]{1,0:T(8,128)(2,1)S(1)} %copy-done.36), channel_id=1, source_target_pairs={{0,1},{1,0},{2,3},{3,2},{4,5},{5,4},{6,7},{7,6},{8,9},{9,8},{10,11... | collective-permute-start | bytes 3145736 | tf_op jit(solution)/shard_map/ppermute | solution.py:620
  75.5 22.5 %copy-start.39 = (bf16[1024,512]{1,0:T(8,128)(2,1)}, bf16[1024,512]{1,0:T(8,128)(2,1)S(1)}, u32[]{:S(2)}) copy-start(bf16[1024,512]{1,0:T(8,128)(2,1)S(1)} %collective-permute-done.1.p_ref) | copy-start | bytes 3145732
  125.4 299.6 %collective-permute-start.4 = (bf16[512,1024]{1,0:T(8,128)(2,1)}, bf16[512,1024]{1,0:T(8,128)(2,1)}, u32[]{:S(2)}, u32[]{:S(2)}) collective-permute-start(bf16[512,1024]{1,0:T(8,128)(2,1)} %convolution_convert_fusion.2), channel_id=1, source_target_pairs={{0,1},{1,0},{2,3},{3,2},{4,5},{5,4},{6,7},{7,6},{8,9},{9,8},{10,11... | collective-permute-start | bytes 3145736 | tf_op jit(solution)/shard_map/ppermute | solution.py:620
  125.7 44.3 %collective-permute-start.5 = (bf16[512,1024]{1,0:T(8,128)(2,1)}, bf16[512,1024]{1,0:T(8,128)(2,1)S(1)}, u32[]{:S(2)}, u32[]{:S(2)}) collective-permute-start(bf16[512,1024]{1,0:T(8,128)(2,1)} %get-tuple-element.55), channel_id=1, source_target_pairs={{0,1},{1,0},{2,3},{3,2},{4,5},{5,4},{6,7},{7,6},{8,9},{9,8},{10,11... | collective-permute-start | bytes 3145736 | tf_op jit(solution)/shard_map/ppermute | solution.py:620
  127.4 42.6 %copy-start.29 = (f32[1024]{0:T(1024)S(1)}, f32[1024]{0:T(1024)}, u32[]{:S(2)}) copy-start(f32[1024]{0:T(1024)} %param.25) | copy-start | bytes 12292
  176.5 27.9 %copy-start.8 = (bf16[512,1024]{1,0:T(8,128)(2,1)}, bf16[512,1024]{1,0:T(8,128)(2,1)S(1)}, u32[]{:S(2)}) copy-start(bf16[512,1024]{1,0:T(8,128)(2,1)S(1)} %get-tuple-element.85.a0_ref) | copy-start | bytes 3145732
  176.5 30.7 %collective-permute-start.6 = (bf16[512,1024]{1,0:T(8,128)(2,1)S(1)}, bf16[512,1024]{1,0:T(8,128)(2,1)}, u32[]{:S(2)}, u32[]{:S(2)}) collective-permute-start(bf16[512,1024]{1,0:T(8,128)(2,1)S(1)} %get-tuple-element.85.a0_ref), channel_id=1, source_target_pairs={{0,1},{1,0},{2,3},{3,2},{4,5},{5,4},{6,7},{7,6},{8,9},{9,8},{10,11... | collective-permute-start | bytes 3145736 | tf_op jit(solution)/shard_map/ppermute | solution.py:620
  188.7 79.8 %collective-permute-start.29 = (bf16[4,1024,256]{2,1,0:T(8,128)(2,1)}, bf16[4,1024,256]{2,1,0:T(8,128)(2,1)}, u32[]{:S(2)}, u32[]{:S(2)}) collective-permute-start(bf16[4,1024,256]{2,1,0:T(8,128)(2,1)} %get-tuple-element.72), channel_id=1, source_target_pairs={{0,2},{2,0},{4,6},{6,4},{8,10},{10,8},{12,14},{14,12},{16,18},{18,... | collective-permute-start | bytes 6291464 | tf_op jit(solution)/shard_map/ppermute | solution.py:398
  192.6 11.8 %copy-start.31 = (f32[1,2048]{1,0:T(1,128)S(1)}, f32[1,2048]{1,0:T(1,128)}, u32[]{:S(2)}) copy-start(f32[1,2048]{1,0:T(1,128)} %get-tuple-element.59) | copy-start | bytes 24580
  192.6 11.8 %copy-start.32 = (f32[1,2048]{1,0:T(1,128)S(1)}, f32[1,2048]{1,0:T(1,128)}, u32[]{:S(2)}) copy-start(f32[1,2048]{1,0:T(1,128)} %get-tuple-element.58) | copy-start | bytes 24580
  204.3 68.6 %collective-permute-start.37 = (bf16[4,256,1024]{2,1,0:T(8,128)(2,1)}, bf16[4,256,1024]{2,1,0:T(8,128)(2,1)}, u32[]{:S(2)}, u32[]{:S(2)}) collective-permute-start(bf16[4,256,1024]{2,1,0:T(8,128)(2,1)} %get-tuple-element.74), channel_id=1, source_target_pairs={{0,2},{2,0},{4,6},{6,4},{8,10},{10,8},{12,14},{14,12},{16,18},{18,... | collective-permute-start | bytes 6291464 | tf_op jit(solution)/shard_map/ppermute | solution.py:398
  245.7 33.6 %collective-permute-start.7 = (bf16[512,1024]{1,0:T(8,128)(2,1)}, bf16[512,1024]{1,0:T(8,128)(2,1)}, u32[]{:S(2)}, u32[]{:S(2)}) collective-permute-start(bf16[512,1024]{1,0:T(8,128)(2,1)} %add_convert_fusion.4), channel_id=1, source_target_pairs={{0,1},{1,0},{2,3},{3,2},{4,5},{5,4},{6,7},{7,6},{8,9},{9,8},{10,11... | collective-permute-start | bytes 3145736 | tf_op jit(solution)/shard_map/ppermute | solution.py:620
  257.1 27.6 %collective-permute-start.13 = (bf16[4,2,128,512]{3,2,1,0:T(8,128)(2,1)}, bf16[4,2,128,512]{3,2,1,0:T(8,128)(2,1)}, u32[]{:S(2)}, u32[]{:S(2)}) collective-permute-start(bf16[4,2,128,512]{3,2,1,0:T(8,128)(2,1)} %get-tuple-element.64), channel_id=1, source_target_pairs={{0,2},{2,0},{4,6},{6,4},{8,10},{10,8},{12,14},{14,12},{16,18},{18,... | collective-permute-start | bytes 3145736 | tf_op jit(solution)/shard_map/ppermute | solution.py:398
  268.5 19.4 %collective-permute-start.21 = (bf16[4,2,128,512]{3,2,1,0:T(8,128)(2,1)}, bf16[4,2,128,512]{3,2,1,0:T(8,128)(2,1)}, u32[]{:S(2)}, u32[]{:S(2)}) collective-permute-start(bf16[4,2,128,512]{3,2,1,0:T(8,128)(2,1)} %get-tuple-element.66), channel_id=1, source_target_pairs={{0,2},{2,0},{4,6},{6,4},{8,10},{10,8},{12,14},{14,12},{16,18},{18,... | collective-permute-start | bytes 3145736 | tf_op jit(solution)/shard_map/ppermute | solution.py:398
  272.9 24.6 %collective-permute-start.30 = (bf16[2,1024,256]{2,1,0:T(8,128)(2,1)}, bf16[2,1024,256]{2,1,0:T(8,128)(2,1)}, u32[]{:S(2)}, u32[]{:S(2)}) collective-permute-start(bf16[2,1024,256]{2,1,0:T(8,128)(2,1)} %get-tuple-element.90), channel_id=1, source_target_pairs={{0,8},{2,10},{4,12},{6,14},{8,0},{10,2},{12,4},{14,6},{16,24},{18,... | collective-permute-start | bytes 3145736 | tf_op jit(solution)/shard_map/ppermute | solution.py:398
  279.3 24.3 %collective-permute-start.38 = (bf16[2,256,1024]{2,1,0:T(8,128)(2,1)}, bf16[2,256,1024]{2,1,0:T(8,128)(2,1)}, u32[]{:S(2)}, u32[]{:S(2)}) collective-permute-start(bf16[2,256,1024]{2,1,0:T(8,128)(2,1)} %get-tuple-element.88), channel_id=1, source_target_pairs={{0,4},{2,6},{4,0},{6,2},{8,12},{10,14},{12,8},{14,10},{16,20},{18,... | collective-permute-start | bytes 3145736 | tf_op jit(solution)/shard_map/ppermute | solution.py:398
  284.7 6.1 %collective-permute-start.8 = (f32[5,1024]{1,0:T(8,128)S(1)}, f32[5,1024]{1,0:T(8,128)S(1)}, u32[]{:S(2)}, u32[]{:S(2)}) collective-permute-start(f32[5,1024]{1,0:T(8,128)S(1)} %stack.40), channel_id=1, source_target_pairs={{0,1},{1,0},{2,3},{3,2},{4,5},{5,4},{6,7},{7,6},{8,9},{9,8},{10,11... | collective-permute-start | bytes 61448 | tf_op jit(solution)/shard_map/ppermute | solution.py:620
  287.9 29.0 %collective-permute-start.14 = (bf16[2,2,128,512]{3,2,1,0:T(8,128)(2,1)}, bf16[2,2,128,512]{3,2,1,0:T(8,128)(2,1)}, u32[]{:S(2)}, u32[]{:S(2)}) collective-permute-start(bf16[2,2,128,512]{3,2,1,0:T(8,128)(2,1)} %get-tuple-element.94), channel_id=1, source_target_pairs={{0,4},{2,6},{4,0},{6,2},{8,12},{10,14},{12,8},{14,10},{16,20},{18,... | collective-permute-start | bytes 1572872 | tf_op jit(solution)/shard_map/ppermute | solution.py:398
  290.8 27.4 %collective-permute-start.22 = (bf16[2,2,128,512]{3,2,1,0:T(8,128)(2,1)}, bf16[2,2,128,512]{3,2,1,0:T(8,128)(2,1)}, u32[]{:S(2)}, u32[]{:S(2)}) collective-permute-start(bf16[2,2,128,512]{3,2,1,0:T(8,128)(2,1)} %get-tuple-element.92), channel_id=1, source_target_pairs={{0,8},{2,10},{4,12},{6,14},{8,0},{10,2},{12,4},{14,6},{16,24},{18,... | collective-permute-start | bytes 1572872 | tf_op jit(solution)/shard_map/ppermute | solution.py:398
  292.1 25.0 %copy-start.17 = (bf16[2,2,128,512]{3,2,1,0:T(8,128)(2,1)S(1)}, bf16[2,2,128,512]{3,2,1,0:T(8,128)(2,1)}, u32[]{:S(2)}) copy-start(bf16[2,2,128,512]{3,2,1,0:T(8,128)(2,1)} %get-tuple-element.93) | copy-start | bytes 1572868
  292.1 27.4 %copy-start.18 = (bf16[2,2,128,512]{3,2,1,0:T(8,128)(2,1)S(1)}, bf16[2,2,128,512]{3,2,1,0:T(8,128)(2,1)}, u32[]{:S(2)}) copy-start(bf16[2,2,128,512]{3,2,1,0:T(8,128)(2,1)} %get-tuple-element.91) | copy-start | bytes 1572868
  297.5 3.7 collective-permute-start.9
  299.8 27.3 %copy-start.12 = (bf16[2,1024,256]{2,1,0:T(8,128)(2,1)S(1)}, bf16[2,1024,256]{2,1,0:T(8,128)(2,1)}, u32[]{:S(2)}) copy-start(bf16[2,1024,256]{2,1,0:T(8,128)(2,1)} %get-tuple-element.89) | copy-start | bytes 3145732
  301.2 25.8 %collective-permute-start.31 = (bf16[1,1024,256]{2,1,0:T(8,128)(2,1)S(1)}, bf16[1,1024,256]{2,1,0:T(8,128)(2,1)S(1)}, u32[]{:S(2)}, u32[]{:S(2)}) collective-permute-start(bf16[1,1024,256]{2,1,0:T(8,128)(2,1)S(1)} %add_convert_fusion.12), channel_id=1, source_target_pairs={{0,16},{2,18},{4,20},{6,22},{8,24},{10,26},{12,28},{14,30},{16,0},... | collective-permute-start | bytes 1572872 | tf_op jit(solution)/shard_map/ppermute | solution.py:398
  303.6 11.9 %collective-permute-start.10 = (f32[58,128]{1,0:T(8,128)S(1)}, f32[58,128]{1,0:T(8,128)S(1)}, u32[]{:S(2)}, u32[]{:S(2)}) collective-permute-start(f32[58,128]{1,0:T(8,128)S(1)} %fusion.42), channel_id=1, source_target_pairs={{0,4},{2,6},{4,0},{6,2},{8,12},{10,14},{12,8},{14,10},{16,20},{18,... | collective-permute-start | bytes 89096 | tf_op jit(solution)/shard_map/ppermute | solution.py:398
  306.2 35.0 %copy-start.13 = (bf16[2,256,1024]{2,1,0:T(8,128)(2,1)S(1)}, bf16[2,256,1024]{2,1,0:T(8,128)(2,1)}, u32[]{:S(2)}) copy-start(bf16[2,256,1024]{2,1,0:T(8,128)(2,1)} %get-tuple-element.87) | copy-start | bytes 3145732
  315.6 24.4 %collective-permute-start.39 = (bf16[1,256,1024]{2,1,0:T(8,128)(2,1)S(1)}, bf16[1,256,1024]{2,1,0:T(8,128)(2,1)S(1)}, u32[]{:S(2)}, u32[]{:S(2)}) collective-permute-start(bf16[1,256,1024]{2,1,0:T(8,128)(2,1)S(1)} %add_convert_fusion.8), channel_id=1, source_target_pairs={{0,8},{2,10},{4,12},{6,14},{8,0},{10,2},{12,4},{14,6},{16,24},{18,... | collective-permute-start | bytes 1572872 | tf_op jit(solution)/shard_map/ppermute | solution.py:398
  316.9 77.2 %collective-permute-start.11 = (f32[58,128]{1,0:T(8,128)S(1)}, f32[58,128]{1,0:T(8,128)S(1)}, u32[]{:S(2)}, u32[]{:S(2)}) collective-permute-start(f32[58,128]{1,0:T(8,128)S(1)} %fusion.60), channel_id=1, source_target_pairs={{0,8},{2,10},{4,12},{6,14},{8,0},{10,2},{12,4},{14,6},{16,24},{18,... | collective-permute-start | bytes 89096 | tf_op jit(solution)/shard_map/ppermute | solution.py:398
  318.2 28.2 %collective-permute-start.15 = (bf16[1,2,128,512]{3,2,1,0:T(8,128)(2,1)S(1)}, bf16[1,2,128,512]{3,2,1,0:T(8,128)(2,1)S(1)}, u32[]{:S(2)}, u32[]{:S(2)}) collective-permute-start(bf16[1,2,128,512]{3,2,1,0:T(8,128)(2,1)S(1)} %add_convert_fusion.24), channel_id=1, source_target_pairs={{0,8},{2,10},{4,12},{6,14},{8,0},{10,2},{12,4},{14,6},{16,24},{18,... | collective-permute-start | bytes 786440 | tf_op jit(solution)/shard_map/ppermute | solution.py:398
  327.1 20.3 %collective-permute-start.23 = (bf16[1,2,128,512]{3,2,1,0:T(8,128)(2,1)S(1)}, bf16[1,2,128,512]{3,2,1,0:T(8,128)(2,1)S(1)}, u32[]{:S(2)}, u32[]{:S(2)}) collective-permute-start(bf16[1,2,128,512]{3,2,1,0:T(8,128)(2,1)S(1)} %add_convert_fusion.20), channel_id=1, source_target_pairs={{0,16},{2,18},{4,20},{6,22},{8,24},{10,26},{12,28},{14,30},{16,0},... | collective-permute-start | bytes 786440 | tf_op jit(solution)/shard_map/ppermute | solution.py:398
  340.0 10.9 %collective-permute-start.32 = (bf16[1,1024,256]{2,1,0:T(8,128)(2,1)S(1)}, bf16[1,1024,256]{2,1,0:T(8,128)(2,1)S(1)}, u32[]{:S(2)}, u32[]{:S(2)}) collective-permute-start(bf16[1,1024,256]{2,1,0:T(8,128)(2,1)S(1)} %add_convert_fusion.11), channel_id=1, source_target_pairs={{0,4},{2,6},{4,0},{6,2},{8,12},{10,14},{12,8},{14,10},{16,20},{18,... | collective-permute-start | bytes 1572872 | tf_op jit(solution)/shard_map/ppermute | solution.py:398
  346.3 47.5 %collective-permute-start.40 = (bf16[1,256,1024]{2,1,0:T(8,128)(2,1)S(1)}, bf16[1,256,1024]{2,1,0:T(8,128)(2,1)S(1)}, u32[]{:S(2)}, u32[]{:S(2)}) collective-permute-start(bf16[1,256,1024]{2,1,0:T(8,128)(2,1)S(1)} %add_convert_fusion.7), channel_id=1, source_target_pairs={{0,16},{2,18},{4,20},{6,22},{8,24},{10,26},{12,28},{14,30},{16,0},... | collective-permute-start | bytes 1572872 | tf_op jit(solution)/shard_map/ppermute | solution.py:398
  347.4 46.4 %collective-permute-start.16 = (bf16[1,2,128,512]{3,2,1,0:T(8,128)(2,1)S(1)}, bf16[1,2,128,512]{3,2,1,0:T(8,128)(2,1)S(1)}, u32[]{:S(2)}, u32[]{:S(2)}) collective-permute-start(bf16[1,2,128,512]{3,2,1,0:T(8,128)(2,1)S(1)} %add_convert_fusion.23), channel_id=1, source_target_pairs={{0,16},{2,18},{4,20},{6,22},{8,24},{10,26},{12,28},{14,30},{16,0},... | collective-permute-start | bytes 786440 | tf_op jit(solution)/shard_map/ppermute | solution.py:398
  350.9 63.1 %collective-permute-start.24 = (bf16[1,2,128,512]{3,2,1,0:T(8,128)(2,1)S(1)}, bf16[1,2,128,512]{3,2,1,0:T(8,128)(2,1)S(1)}, u32[]{:S(2)}, u32[]{:S(2)}) collective-permute-start(bf16[1,2,128,512]{3,2,1,0:T(8,128)(2,1)S(1)} %add_convert_fusion.19), channel_id=1, source_target_pairs={{0,4},{2,6},{4,0},{6,2},{8,12},{10,14},{12,8},{14,10},{16,20},{18,... | collective-permute-start | bytes 786440 | tf_op jit(solution)/shard_map/ppermute | solution.py:398
  393.7 22.6 %collective-permute-start.33 = (bf16[1,1024,256]{2,1,0:T(8,128)(2,1)S(1)}, bf16[1,1024,256]{2,1,0:T(8,128)(2,1)S(1)}, u32[]{:S(2)}, u32[]{:S(2)}) collective-permute-start(bf16[1,1024,256]{2,1,0:T(8,128)(2,1)S(1)} %add_convert_fusion.10), channel_id=1, source_target_pairs={{0,16},{2,18},{4,20},{6,22},{8,24},{10,26},{12,28},{14,30},{16,0},... | collective-permute-start | bytes 1572872 | tf_op jit(solution)/shard_map/ppermute | solution.py:398
  393.8 18.8 %collective-permute-start.17 = (bf16[1,2,128,512]{3,2,1,0:T(8,128)(2,1)S(1)}, bf16[1,2,128,512]{3,2,1,0:T(8,128)(2,1)S(1)}, u32[]{:S(2)}, u32[]{:S(2)}) collective-permute-start(bf16[1,2,128,512]{3,2,1,0:T(8,128)(2,1)S(1)} %add_convert_fusion.22), channel_id=1, source_target_pairs={{0,8},{2,10},{4,12},{6,14},{8,0},{10,2},{12,4},{14,6},{16,24},{18,... | collective-permute-start | bytes 786440 | tf_op jit(solution)/shard_map/ppermute | solution.py:398
  394.1 29.8 %collective-permute-start.41 = (bf16[1,256,1024]{2,1,0:T(8,128)(2,1)S(1)}, bf16[1,256,1024]{2,1,0:T(8,128)(2,1)S(1)}, u32[]{:S(2)}, u32[]{:S(2)}) collective-permute-start(bf16[1,256,1024]{2,1,0:T(8,128)(2,1)S(1)} %add_convert_fusion.6), channel_id=1, source_target_pairs={{0,8},{2,10},{4,12},{6,14},{8,0},{10,2},{12,4},{14,6},{16,24},{18,... | collective-permute-start | bytes 1572872 | tf_op jit(solution)/shard_map/ppermute | solution.py:398
  412.6 23.4 %copy-start.42 = (bf16[512,2048]{1,0:T(8,128)(2,1)S(1)}, bf16[512,2048]{1,0:T(8,128)(2,1)}, u32[]{:S(2)}) copy-start(bf16[512,2048]{1,0:T(8,128)(2,1)} %get-tuple-element.51.a0_ref) | copy-start | bytes 6291460
  412.7 12.4 %copy-start.14 = (bf16[2,2,128,512]{3,2,1,0:T(8,128)(2,1)}, bf16[2,2,128,512]{3,2,1,0:T(8,128)(2,1)S(1)}, u32[]{:S(2)}) copy-start(bf16[2,2,128,512]{3,2,1,0:T(8,128)(2,1)S(1)} %pad_maximum_fusion.2.refs_0_) | copy-start | bytes 1572868
  412.7 19.3 %collective-permute-start.18 = (bf16[2,2,128,512]{3,2,1,0:T(8,128)(2,1)S(1)}, bf16[2,2,128,512]{3,2,1,0:T(8,128)(2,1)S(1)}, u32[]{:S(2)}, u32[]{:S(2)}) collective-permute-start(bf16[2,2,128,512]{3,2,1,0:T(8,128)(2,1)S(1)} %pad_maximum_fusion.2.refs_0_), channel_id=1, source_target_pairs={{0,4},{2,6},{4,0},{6,2},{8,12},{10,14},{12,8},{14,10},{16,20},{18,... | collective-permute-start | bytes 1572872 | tf_op jit(solution)/shard_map/ppermute | solution.py:398
  414.0 22.0 %collective-permute-start.19 = (bf16[2,2,128,512]{3,2,1,0:T(8,128)(2,1)S(1)}, bf16[2,2,128,512]{3,2,1,0:T(8,128)(2,1)S(1)}, u32[]{:S(2)}, u32[]{:S(2)}) collective-permute-start(bf16[2,2,128,512]{3,2,1,0:T(8,128)(2,1)S(1)} %pad_maximum_fusion.2.refs_0_), channel_id=1, source_target_pairs={{0,2},{2,0},{4,6},{6,4},{8,10},{10,8},{12,14},{14,12},{16,18},{18,... | collective-permute-start | bytes 1572872 | tf_op jit(solution)/shard_map/ppermute | solution.py:398
  416.4 14.9 %collective-permute-start.25 = (bf16[1,2,128,512]{3,2,1,0:T(8,128)(2,1)S(1)}, bf16[1,2,128,512]{3,2,1,0:T(8,128)(2,1)S(1)}, u32[]{:S(2)}, u32[]{:S(2)}) collective-permute-start(bf16[1,2,128,512]{3,2,1,0:T(8,128)(2,1)S(1)} %add_convert_fusion.18), channel_id=1, source_target_pairs={{0,16},{2,18},{4,20},{6,22},{8,24},{10,26},{12,28},{14,30},{16,0},... | collective-permute-start | bytes 786440 | tf_op jit(solution)/shard_map/ppermute | solution.py:398
  416.5 19.6 %copy-start.35 = (bf16[2048,1024]{1,0:T(8,128)(2,1)S(1)}, bf16[2048,1024]{1,0:T(8,128)(2,1)}, u32[]{:S(2)}) copy-start(bf16[2048,1024]{1,0:T(8,128)(2,1)} %param.29) | copy-start | bytes 12582916
  417.5 18.5 %copy-start.41 = (f32[1024]{0:T(1024)S(1)}, f32[1024]{0:T(1024)}, u32[]{:S(2)}) copy-start(f32[1024]{0:T(1024)} %param.30) | copy-start | bytes 12292
  424.0 8.1 %collective-permute-start.12 = (f32[58,128]{1,0:T(8,128)S(1)}, f32[58,128]{1,0:T(8,128)S(1)}, u32[]{:S(2)}, u32[]{:S(2)}) collective-permute-start(f32[58,128]{1,0:T(8,128)S(1)} %add.234), channel_id=1, source_target_pairs={{0,16},{2,18},{4,20},{6,22},{8,24},{10,26},{12,28},{14,30},{16,0},... | collective-permute-start | bytes 89096 | tf_op jit(solution)/shard_map/ppermute | solution.py:398
  425.0 41.0 %collective-permute-start.34 = (bf16[2,1024,256]{2,1,0:T(8,128)(2,1)}, bf16[2,1024,256]{2,1,0:T(8,128)(2,1)}, u32[]{:S(2)}, u32[]{:S(2)}) collective-permute-start(bf16[2,1024,256]{2,1,0:T(8,128)(2,1)} %pad_maximum_fusion.refs_0_), channel_id=1, source_target_pairs={{0,8},{2,10},{4,12},{6,14},{8,0},{10,2},{12,4},{14,6},{16,24},{18,... | collective-permute-start | bytes 3145736 | tf_op jit(solution)/shard_map/ppermute | solution.py:398
  431.3 35.1 %collective-permute-start.42 = (bf16[2,256,1024]{2,1,0:T(8,128)(2,1)}, bf16[2,256,1024]{2,1,0:T(8,128)(2,1)}, u32[]{:S(2)}, u32[]{:S(2)}) collective-permute-start(bf16[2,256,1024]{2,1,0:T(8,128)(2,1)} %pad_maximum_fusion.1.refs_0_), channel_id=1, source_target_pairs={{0,4},{2,6},{4,0},{6,2},{8,12},{10,14},{12,8},{14,10},{16,20},{18,... | collective-permute-start | bytes 3145736 | tf_op jit(solution)/shard_map/ppermute | solution.py:398
  431.4 9.4 %copy-start.15 = (bf16[2,2,128,512]{3,2,1,0:T(8,128)(2,1)}, bf16[2,2,128,512]{3,2,1,0:T(8,128)(2,1)S(1)}, u32[]{:S(2)}) copy-start(bf16[2,2,128,512]{3,2,1,0:T(8,128)(2,1)S(1)} %pad_maximum_fusion.3.refs_1_) | copy-start | bytes 1572868
  431.4 35.6 %copy-start.6 = (f32[512,1024]{1,0:T(8,128)S(1)}, f32[512,1024]{1,0:T(8,128)}, u32[]{:S(2)}) copy-start(f32[512,1024]{1,0:T(8,128)} %get-tuple-element.86) | copy-start | bytes 6291460
  431.4 35.6 %copy-start.16 = (f32[512,1024]{1,0:T(8,128)S(1)}, f32[512,1024]{1,0:T(8,128)}, u32[]{:S(2)}) copy-start(f32[512,1024]{1,0:T(8,128)} %get-tuple-element.100) | copy-start | bytes 6291460
  432.0 33.3 %collective-permute-start.26 = (bf16[2,2,128,512]{3,2,1,0:T(8,128)(2,1)S(1)}, bf16[2,2,128,512]{3,2,1,0:T(8,128)(2,1)}, u32[]{:S(2)}, u32[]{:S(2)}) collective-permute-start(bf16[2,2,128,512]{3,2,1,0:T(8,128)(2,1)S(1)} %pad_maximum_fusion.3.refs_1_), channel_id=1, source_target_pairs={{0,8},{2,10},{4,12},{6,14},{8,0},{10,2},{12,4},{14,6},{16,24},{18,... | collective-permute-start | bytes 1572872 | tf_op jit(solution)/shard_map/ppermute | solution.py:398
  432.0 8.7 %copy-start.24 = (bf16[2,2,128,512]{3,2,1,0:T(8,128)(2,1)}, bf16[2,2,128,512]{3,2,1,0:T(8,128)(2,1)S(1)}, u32[]{:S(2)}) copy-start(bf16[2,2,128,512]{3,2,1,0:T(8,128)(2,1)S(1)} %collective-permute-done.18.refs_1_) | copy-start | bytes 1572868
  432.0 33.9 %collective-permute-start.27 = (bf16[2,2,128,512]{3,2,1,0:T(8,128)(2,1)S(1)}, bf16[2,2,128,512]{3,2,1,0:T(8,128)(2,1)S(1)}, u32[]{:S(2)}, u32[]{:S(2)}) collective-permute-start(bf16[2,2,128,512]{3,2,1,0:T(8,128)(2,1)S(1)} %pad_maximum_fusion.3.refs_1_), channel_id=1, source_target_pairs={{0,2},{2,0},{4,6},{6,4},{8,10},{10,8},{12,14},{14,12},{16,18},{18,... | collective-permute-start | bytes 1572872 | tf_op jit(solution)/shard_map/ppermute | solution.py:398
  436.0 30.6 %collective-permute-start.20 = (bf16[2,2,128,512]{3,2,1,0:T(8,128)(2,1)S(1)}, bf16[2,2,128,512]{3,2,1,0:T(8,128)(2,1)S(1)}, u32[]{:S(2)}, u32[]{:S(2)}) collective-permute-start(bf16[2,2,128,512]{3,2,1,0:T(8,128)(2,1)S(1)} %collective-permute-done.18.refs_1_), channel_id=1, source_target_pairs={{0,2},{2,0},{4,6},{6,4},{8,10},{10,8},{12,14},{14,12},{16,18},{18,... | collective-permute-start | bytes 1572872 | tf_op jit(solution)/shard_map/ppermute | solution.py:398
  465.3 19.7 %collective-permute-start.35 = (bf16[2,1024,256]{2,1,0:T(8,128)(2,1)}, bf16[2,1024,256]{2,1,0:T(8,128)(2,1)S(1)}, u32[]{:S(2)}, u32[]{:S(2)}) collective-permute-start(bf16[2,1024,256]{2,1,0:T(8,128)(2,1)} %pad_maximum_fusion.refs_0_), channel_id=1, source_target_pairs={{0,2},{2,0},{4,6},{6,4},{8,10},{10,8},{12,14},{14,12},{16,18},{18,... | collective-permute-start | bytes 3145736 | tf_op jit(solution)/shard_map/ppermute | solution.py:398
  465.9 28.7 %collective-permute-start.43 = (bf16[2,256,1024]{2,1,0:T(8,128)(2,1)}, bf16[2,256,1024]{2,1,0:T(8,128)(2,1)S(1)}, u32[]{:S(2)}, u32[]{:S(2)}) collective-permute-start(bf16[2,256,1024]{2,1,0:T(8,128)(2,1)} %pad_maximum_fusion.1.refs_0_), channel_id=1, source_target_pairs={{0,2},{2,0},{4,6},{6,4},{8,10},{10,8},{12,14},{14,12},{16,18},{18,... | collective-permute-start | bytes 3145736 | tf_op jit(solution)/shard_map/ppermute | solution.py:398
  466.0 19.0 %collective-permute-start.36 = (bf16[2,1024,256]{2,1,0:T(8,128)(2,1)}, bf16[2,1024,256]{2,1,0:T(8,128)(2,1)}, u32[]{:S(2)}, u32[]{:S(2)}) collective-permute-start(bf16[2,1024,256]{2,1,0:T(8,128)(2,1)} %collective-permute-done.34.refs_1_), channel_id=1, source_target_pairs={{0,2},{2,0},{4,6},{6,4},{8,10},{10,8},{12,14},{14,12},{16,18},{18,... | collective-permute-start | bytes 3145736 | tf_op jit(solution)/shard_map/ppermute | solution.py:398
  466.4 28.2 %collective-permute-start.44 = (bf16[2,256,1024]{2,1,0:T(8,128)(2,1)}, bf16[2,256,1024]{2,1,0:T(8,128)(2,1)}, u32[]{:S(2)}, u32[]{:S(2)}) collective-permute-start(bf16[2,256,1024]{2,1,0:T(8,128)(2,1)} %collective-permute-done.42.refs_1_), channel_id=1, source_target_pairs={{0,2},{2,0},{4,6},{6,4},{8,10},{10,8},{12,14},{14,12},{16,18},{18,... | collective-permute-start | bytes 3145736 | tf_op jit(solution)/shard_map/ppermute | solution.py:398
  466.5 11.2 %collective-permute-start.28 = (bf16[2,2,128,512]{3,2,1,0:T(8,128)(2,1)}, bf16[2,2,128,512]{3,2,1,0:T(8,128)(2,1)}, u32[]{:S(2)}, u32[]{:S(2)}) collective-permute-start(bf16[2,2,128,512]{3,2,1,0:T(8,128)(2,1)} %collective-permute-done.26.refs_2_), channel_id=1, source_target_pairs={{0,2},{2,0},{4,6},{6,4},{8,10},{10,8},{12,14},{14,12},{16,18},{18,... | collective-permute-start | bytes 1572872 | tf_op jit(solution)/shard_map/ppermute | solution.py:398
  (24 other events, 84.8 us)
